TPU v7x, 32 devices: a whole 2x2x4 slice. The times are simulated.
32 devices in a mesh: dp: 4 (over y, x), tensor: 8 (over z, core).
Axes of the slice: x: 2, y: 2, z: 4, core: 2. Of those that a mesh axis runs over, the one named last changes fastest.
Arguments:
- latents: bfloat16 [4, 2048, 1152], P('dp', 'tensor'), may hold values from -6 to 6
- conditioning: bfloat16 [4, 1152], P('dp', 'tensor'), may hold values from -6 to 6
- ada_weight: bfloat16 [2, 1152, 6912], P(None, 'tensor'), may hold values from -0.1875 to 0.1875
- ada_bias: bfloat16 [2, 6912], replicated, may hold values from -3 to 3
- qkv_weight: bfloat16 [2, 1152, 3, 1152], P(None, None, None, 'tensor'), may hold values from -0.1875 to 0.1875
- qkv_bias: bfloat16 [2, 2, 1152], P(None, None, 'tensor'), may hold values from -3 to 3
- out_weight: bfloat16 [2, 1152, 1152], P(None, 'tensor'), may hold values from -0.75 to 0.75
- out_bias: bfloat16 [2, 1152], replicated, may hold values from -3 to 3
- fc1_weight: bfloat16 [2, 1152, 4608], P(None, None, 'tensor'), may hold values from -0.1875 to 0.1875
- fc1_bias: bfloat16 [2, 4608], P(None, 'tensor'), may hold values from -3 to 3
- fc2_weight: bfloat16 [2, 4608, 1152], P(None, 'tensor'), may hold values from -0.09375 to 0.09375
- fc2_bias: bfloat16 [2, 1152], replicated, may hold values from -3 to 3
- out_grad: bfloat16 [4, 2048, 1152], P('dp', 'tensor'), may hold values from -6 to 6
Outputs:
- layer_output: bfloat16 [4, 2048, 1152], P('dp', 'tensor')
- latents_grad: bfloat16 [4, 2048, 1152], P('dp', 'tensor')
- conditioning_grad: bfloat16 [4, 1152], P('dp', 'tensor')
- ada_weight_grad: float32 [2, 1152, 6912], P(None, 'tensor')
- ada_bias_grad: float32 [2, 6912], replicated
- qkv_weight_grad: float32 [2, 1152, 3, 1152], P(None, None, None, 'tensor')
- qkv_bias_grad: float32 [2, 2, 1152], P(None, None, 'tensor')
- out_weight_grad: float32 [2, 1152, 1152], P(None, 'tensor')
- out_bias_grad: float32 [2, 1152], replicated
- fc1_weight_grad: float32 [2, 1152, 4608], P(None, None, 'tensor')
- fc1_bias_grad: float32 [2, 4608], P(None, 'tensor')
- fc2_weight_grad: float32 [2, 4608, 1152], P(None, 'tensor')
- fc2_bias_grad: float32 [2, 1152], replicated
All inputs are finite; a program needn't handle non-finite values.
Results may differ from a plain program's by a relative error of at most 0.04.
Values may be sent and summed in bfloat16 or wider, within the bound.
A program may use at most 256 MiB of HBM per device.

v0:
```python
from functools import partial

import jax
import jax.numpy as jnp
from jax import lax
from jax.sharding import PartitionSpec as P

HEAD_DIM = 72
PATCHES = 256
FRAMES = 8
LAYERS = 2


def normalize(stream):
    centered = stream - jnp.mean(stream, axis=-1, keepdims=True)
    variance = jnp.mean(centered * centered, axis=-1, keepdims=True)
    return centered * lax.rsqrt(variance + 1e-06)


def modulate(stream, shift_in, scale_in):
    return normalize(stream) * (1.0 + scale_in) + shift_in


def grouped(token_rows, spatial):
    heads_here = token_rows.shape[1] // HEAD_DIM
    shaped = token_rows.reshape(FRAMES, PATCHES, heads_here, HEAD_DIM)
    if spatial:
        return shaped
    return jnp.transpose(shaped, (1, 0, 2, 3))


def ungrouped(groups, spatial):
    if not spatial:
        groups = jnp.transpose(groups, (1, 0, 2, 3))
    return groups.reshape(FRAMES * PATCHES, groups.shape[2] * HEAD_DIM)


def softmax_rows(query_g, key_g):
    scores = jnp.einsum(
        "gqhd,gkhd->ghqk", query_g, key_g, preferred_element_type=jnp.float32
    ) * HEAD_DIM ** (-0.5)
    return jax.nn.softmax(scores, axis=-1)


def attend(query_rows, key_rows, value_rows, spatial):
    attn_probs = softmax_rows(grouped(query_rows, spatial), grouped(key_rows, spatial)).astype(
        jnp.bfloat16
    )
    mixed = jnp.einsum(
        "ghqk,gkhd->gqhd",
        attn_probs,
        grouped(value_rows, spatial),
        preferred_element_type=jnp.float32,
    )
    return ungrouped(mixed, spatial)


def attend_back(query_rows, key_rows, value_rows, mixed_grad, spatial):
    query_g = grouped(query_rows, spatial)
    key_g = grouped(key_rows, spatial)
    value_g = grouped(value_rows, spatial)
    grad_g = grouped(mixed_grad, spatial)
    probs_full = softmax_rows(query_g, key_g)
    value_grad = jnp.einsum(
        "ghqk,gqhd->gkhd",
        probs_full.astype(jnp.bfloat16),
        grad_g,
        preferred_element_type=jnp.float32,
    )
    probs_grad = jnp.einsum("gqhd,gkhd->ghqk", grad_g, value_g, preferred_element_type=jnp.float32)
    score_grad = probs_full * (
        probs_grad - jnp.sum(probs_grad * probs_full, axis=-1, keepdims=True)
    )
    score_low = score_grad.astype(jnp.bfloat16)
    factor = HEAD_DIM ** (-0.5)
    query_grad = (
        jnp.einsum("ghqk,gkhd->gqhd", score_low, key_g, preferred_element_type=jnp.float32) * factor
    )
    key_grad = (
        jnp.einsum("ghqk,gqhd->gkhd", score_low, query_g, preferred_element_type=jnp.float32)
        * factor
    )
    return (
        ungrouped(query_grad, spatial),
        ungrouped(key_grad, spatial),
        ungrouped(value_grad, spatial),
    )


def spread_rows(row_block):
    return lax.all_gather(row_block, "tensor", axis=0, tiled=True)


def reduce_rows(partial_terms):
    return lax.psum_scatter(
        partial_terms.astype(jnp.bfloat16), "tensor", scatter_dimension=0, tiled=True
    ).astype(jnp.float32)


def spread_grads(row_block):
    return lax.all_gather(row_block, "tensor", axis=0, tiled=True)


def reduce_grads(partial_terms):
    return lax.psum_scatter(
        partial_terms.astype(jnp.bfloat16), "tensor", scatter_dimension=0, tiled=True
    ).astype(jnp.float32)


def layer_forward(stream, modulation, params, spatial):
    qkv_w, qkv_b, out_w, out_b, fc1_w, fc1_b, fc2_w, fc2_b = params
    shift_att, scale_att, gate_att, shift_mlp, scale_mlp, gate_mlp = jnp.split(modulation, 6)
    normed = spread_rows(modulate(stream, shift_att, scale_att).astype(jnp.bfloat16))
    head_width = qkv_w.shape[2]
    projected = jnp.dot(
        normed, qkv_w.reshape(qkv_w.shape[0], 3 * head_width), preferred_element_type=jnp.float32
    )
    query_rows = (projected[:, :head_width] + qkv_b[0].astype(jnp.float32)).astype(jnp.bfloat16)
    key_rows = projected[:, head_width : 2 * head_width].astype(jnp.bfloat16)
    value_rows = (projected[:, 2 * head_width :] + qkv_b[1].astype(jnp.float32)).astype(
        jnp.bfloat16
    )
    heads_out = attend(query_rows, key_rows, value_rows, spatial).astype(jnp.bfloat16)
    attn_branch = reduce_rows(
        jnp.dot(heads_out, out_w, preferred_element_type=jnp.float32)
    ) + out_b.astype(jnp.float32)
    middle = stream + gate_att * attn_branch
    normed_mlp = spread_rows(modulate(middle, shift_mlp, scale_mlp).astype(jnp.bfloat16))
    hidden = jnp.dot(normed_mlp, fc1_w, preferred_element_type=jnp.float32) + fc1_b.astype(
        jnp.float32
    )
    activated = jax.nn.gelu(hidden, approximate=True).astype(jnp.bfloat16)
    mlp_branch = reduce_rows(
        jnp.dot(activated, fc2_w, preferred_element_type=jnp.float32)
    ) + fc2_b.astype(jnp.float32)
    result = middle + gate_mlp * mlp_branch
    saved = (
        normed,
        query_rows,
        key_rows,
        value_rows,
        heads_out,
        attn_branch,
        middle,
        normed_mlp,
        hidden,
        mlp_branch,
    )
    return (result, saved)


def layer_backward(stream, modulation, params, saved, stream_grad, spatial):
    qkv_w, qkv_b, out_w, out_b, fc1_w, fc1_b, fc2_w, fc2_b = params
    (
        normed,
        query_rows,
        key_rows,
        value_rows,
        heads_out,
        attn_branch,
        middle,
        normed_mlp,
        hidden,
        mlp_branch,
    ) = saved
    shift_att, scale_att, gate_att, shift_mlp, scale_mlp, gate_mlp = jnp.split(modulation, 6)
    head_width = qkv_w.shape[2]
    mlp_grad = (gate_mlp * stream_grad).astype(jnp.bfloat16)
    gate_mlp_grad = jnp.sum(stream_grad * mlp_branch, axis=0)
    fc2_b_grad = jnp.sum(mlp_grad, axis=0, dtype=jnp.float32)
    mlp_grad_all = spread_grads(mlp_grad)
    gelu_out, gelu_back = jax.vjp(partial(jax.nn.gelu, approximate=True), hidden)
    activated = gelu_out.astype(jnp.bfloat16)
    fc2_w_grad = jnp.einsum(
        "tf,td->fd", activated, mlp_grad_all, preferred_element_type=jnp.float32
    )
    act_grad = jnp.einsum("td,fd->tf", mlp_grad_all, fc2_w, preferred_element_type=jnp.float32)
    hidden_grad = gelu_back(act_grad)[0].astype(jnp.bfloat16)
    fc1_b_grad = jnp.sum(hidden_grad, axis=0, dtype=jnp.float32)
    fc1_w_grad = jnp.einsum(
        "td,tf->df", normed_mlp, hidden_grad, preferred_element_type=jnp.float32
    )
    mlp_in_grad = reduce_grads(
        jnp.einsum("tf,df->td", hidden_grad, fc1_w, preferred_element_type=jnp.float32)
    )
    _, mlp_norm_back = jax.vjp(modulate, middle, shift_mlp, scale_mlp)
    middle_part, shift_mlp_grad, scale_mlp_grad = mlp_norm_back(mlp_in_grad)
    middle_grad = stream_grad + middle_part
    attn_grad = (gate_att * middle_grad).astype(jnp.bfloat16)
    gate_att_grad = jnp.sum(middle_grad * attn_branch, axis=0)
    out_b_grad = jnp.sum(attn_grad, axis=0, dtype=jnp.float32)
    attn_grad_all = spread_grads(attn_grad)
    out_w_grad = jnp.einsum(
        "tw,td->wd", heads_out, attn_grad_all, preferred_element_type=jnp.float32
    )
    heads_grad = jnp.einsum(
        "td,wd->tw", attn_grad_all, out_w, preferred_element_type=jnp.float32
    ).astype(jnp.bfloat16)
    query_grad, key_grad, value_grad = attend_back(
        query_rows, key_rows, value_rows, heads_grad, spatial
    )
    qkv_grad = jnp.concatenate([query_grad, key_grad, value_grad], axis=1).astype(jnp.bfloat16)
    qkv_b_grad = jnp.stack(
        [
            jnp.sum(qkv_grad[:, :head_width], axis=0, dtype=jnp.float32),
            jnp.sum(qkv_grad[:, 2 * head_width :], axis=0, dtype=jnp.float32),
        ]
    )
    qkv_flat = qkv_w.reshape(qkv_w.shape[0], 3 * head_width)
    qkv_w_grad = jnp.einsum(
        "td,tw->dw", normed, qkv_grad, preferred_element_type=jnp.float32
    ).reshape(qkv_w.shape)
    attn_in_grad = reduce_grads(
        jnp.einsum("tw,dw->td", qkv_grad, qkv_flat, preferred_element_type=jnp.float32)
    )
    _, att_norm_back = jax.vjp(modulate, stream, shift_att, scale_att)
    stream_part, shift_att_grad, scale_att_grad = att_norm_back(attn_in_grad)
    input_grad = middle_grad + stream_part
    modulation_grad = jnp.concatenate(
        [
            shift_att_grad,
            scale_att_grad,
            gate_att_grad,
            shift_mlp_grad,
            scale_mlp_grad,
            gate_mlp_grad,
        ]
    )
    return (
        input_grad,
        modulation_grad,
        (
            qkv_w_grad,
            qkv_b_grad,
            out_w_grad,
            out_b_grad,
            fc1_w_grad,
            fc1_b_grad,
            fc2_w_grad,
            fc2_b_grad,
        ),
    )


def per_device(
    latents,
    conditioning,
    ada_weight,
    ada_bias,
    qkv_weight,
    qkv_bias,
    out_weight,
    out_bias,
    fc1_weight,
    fc1_bias,
    fc2_weight,
    fc2_bias,
    out_grad,
):
    cond_row = conditioning[0].astype(jnp.float32)
    silu_out, silu_back = jax.vjp(jax.nn.silu, cond_row)
    silu_cond = silu_out.astype(jnp.bfloat16)
    ada_terms = jnp.einsum("d,ldm->lm", silu_cond, ada_weight, preferred_element_type=jnp.float32)
    modulations = lax.psum(ada_terms, "tensor") + ada_bias.astype(jnp.float32)
    stacked = (
        qkv_weight,
        qkv_bias,
        out_weight,
        out_bias,
        fc1_weight,
        fc1_bias,
        fc2_weight,
        fc2_bias,
    )
    stream = latents[0].astype(jnp.float32)
    inputs_kept = []
    saved_all = []
    for layer_idx in range(LAYERS):
        params = tuple((member[layer_idx] for member in stacked))
        inputs_kept.append(stream)
        stream, saved = layer_forward(stream, modulations[layer_idx], params, layer_idx % 2 == 0)
        saved_all.append(saved)
    layer_output = stream.astype(jnp.bfloat16)[None]
    stream_grad = out_grad[0].astype(jnp.float32)
    mod_grads = [None] * LAYERS
    layer_grads = [None] * LAYERS
    for layer_idx in reversed(range(LAYERS)):
        params = tuple((member[layer_idx] for member in stacked))
        spatial = layer_idx % 2 == 0
        saved = layer_forward(inputs_kept[layer_idx], modulations[layer_idx], params, spatial)[1]
        stream_grad, mod_grads[layer_idx], layer_grads[layer_idx] = layer_backward(
            inputs_kept[layer_idx], modulations[layer_idx], params, saved, stream_grad, spatial
        )

    def collect(position):
        return jnp.stack([member[position] for member in layer_grads])

    mod_sum, out_b_sum, fc2_b_sum = (
        lax.psum(jnp.stack(mod_grads).astype(jnp.bfloat16), "tensor").astype(jnp.float32),
        lax.psum(collect(3).astype(jnp.bfloat16), "tensor").astype(jnp.float32),
        lax.psum(collect(7).astype(jnp.bfloat16), "tensor").astype(jnp.float32),
    )
    mod_low = mod_sum.astype(jnp.bfloat16)
    ada_w_grad = (
        silu_cond.astype(jnp.float32)[None, :, None] * mod_low.astype(jnp.float32)[:, None, :]
    )
    ada_b_grad = mod_low.astype(jnp.float32)
    silu_grad = jnp.einsum("lm,ldm->d", mod_low, ada_weight, preferred_element_type=jnp.float32)
    cond_grad = silu_back(silu_grad)[0]
    summed = (
        lax.psum(ada_w_grad.astype(jnp.bfloat16), "dp").astype(jnp.float32),
        lax.psum(ada_b_grad.astype(jnp.bfloat16), "dp").astype(jnp.float32),
        lax.psum(collect(0).astype(jnp.bfloat16), "dp").astype(jnp.float32),
        lax.psum(collect(1).astype(jnp.bfloat16), "dp").astype(jnp.float32),
        lax.psum(collect(2).astype(jnp.bfloat16), "dp").astype(jnp.float32),
        lax.psum(out_b_sum.astype(jnp.bfloat16), "dp").astype(jnp.float32),
        lax.psum(collect(4).astype(jnp.bfloat16), "dp").astype(jnp.float32),
        lax.psum(collect(5).astype(jnp.bfloat16), "dp").astype(jnp.float32),
        lax.psum(collect(6).astype(jnp.bfloat16), "dp").astype(jnp.float32),
        lax.psum(fc2_b_sum.astype(jnp.bfloat16), "dp").astype(jnp.float32),
    )
    return (
        layer_output,
        stream_grad.astype(jnp.bfloat16)[None],
        cond_grad.astype(jnp.bfloat16)[None],
        summed[0],
        summed[1],
        summed[2],
        summed[3],
        summed[4],
        summed[5],
        summed[6],
        summed[7],
        summed[8],
        summed[9],
    )


def solution(mesh):
    in_specs = (
        P("dp", "tensor", None),
        P("dp", "tensor"),
        P(None, "tensor", None),
        P(),
        P(None, None, None, "tensor"),
        P(None, None, "tensor"),
        P(None, "tensor", None),
        P(),
        P(None, None, "tensor"),
        P(None, "tensor"),
        P(None, "tensor", None),
        P(),
        P("dp", "tensor", None),
    )
    out_specs = (
        P("dp", "tensor", None),
        P("dp", "tensor", None),
        P("dp", "tensor"),
        P(None, "tensor", None),
        P(),
        P(None, None, None, "tensor"),
        P(None, None, "tensor"),
        P(None, "tensor", None),
        P(),
        P(None, None, "tensor"),
        P(None, "tensor"),
        P(None, "tensor", None),
        P(),
    )
    return jax.shard_map(
        per_device, mesh=mesh, in_specs=in_specs, out_specs=out_specs, check_vma=False
    )
```

profile of v0, /device:TPU:0, one launch (start us, length us, event | category | flops | bytes accessed | tf_op | source)
XLA Modules:
  0.0 1360.1 jit_solution(16830422912774858308)
XLA Ops:
  11.1 2.8 fusion.180
  14.0 30.9 %psum.98 = f32[2,6912]{1,0:T(2,128)S(1)} all-reduce(f32[2,6912]{1,0:T(2,128)S(1)} %bitcast.362), channel_id=1, replica_groups=mesh['dp'=4,'tensor'=8] {'tensor'}, use_global_device_ids=true, to_apply=%region_0.1 | all-reduce | flops 13824 | bytes 110592 | tf_op jit(solution)/shard_map/psum | solution.py:264
  48.3 48.6 %all-gather.9.cloned.1.call-done = bf16[2048,1152]{1,0:T(8,128)(2,1)} async-done(((bf16[256,1152]{1,0:T(8,128)(2,1)}), bf16[2048,1152]{1,0:T(8,128)(2,1)}) %all-gather.9.cloned.1.call-update) | async-done | bytes 4718608 | tf_op jit(solution)/shard_map/all_gather | solution.py:91
  96.8 5.1 fusion.181
  104.4 3.2 fusion.168
  110.7 3.8 convolution_convert_fusion.7
  115.8 52.6 %reduce-scatter.9.cloned.1.call-done = bf16[256,1152]{1,0:T(8,128)(2,1)} async-done(((bf16[2048,1152]{1,0:T(8,128)(2,1)}), bf16[256,1152]{1,0:T(8,128)(2,1)}) %reduce-scatter.9.cloned.1.call-update) | async-done | bytes 589840 | tf_op jit(solution)/shard_map/reduce_scatter | solution.py:95
  173.6 49.3 %all-gather.11.cloned.1.call-done = bf16[2048,1152]{1,0:T(8,128)(2,1)} async-done(((bf16[256,1152]{1,0:T(8,128)(2,1)}), bf16[2048,1152]{1,0:T(8,128)(2,1)}) %all-gather.11.cloned.1.call-update) | async-done | bytes 4718608 | tf_op jit(solution)/shard_map/all_gather | solution.py:91
  223.0 5.6 fusion.59
  228.7 2.2 copy-done.121
  230.9 6.7 convolution_convert_fusion.6
  238.9 52.6 %reduce-scatter.11.cloned.1.call-done = bf16[256,1152]{1,0:T(8,128)(2,1)} async-done(((bf16[2048,1152]{1,0:T(8,128)(2,1)}), bf16[256,1152]{1,0:T(8,128)(2,1)}) %reduce-scatter.11.cloned.1.call-update) | async-done | bytes 589840 | tf_op jit(solution)/shard_map/reduce_scatter | solution.py:95
  294.5 50.2 %all-gather.13.cloned.1.call-done = bf16[2048,1152]{1,0:T(8,128)(2,1)} async-done(((bf16[256,1152]{1,0:T(8,128)(2,1)}), bf16[2048,1152]{1,0:T(8,128)(2,1)}) %all-gather.13.cloned.1.call-update) | async-done | bytes 4718608 | tf_op jit(solution)/shard_map/all_gather | solution.py:91
  344.7 4.8 fusion.182
  356.7 5.3 fusion.169
  362.0 3.7 fusion.40
  368.6 4.8 convolution_convert_fusion.5
  373.4 53.9 %reduce-scatter.13.cloned.1.call-done = bf16[256,1152]{1,0:T(8,128)(2,1)} async-done(((bf16[2048,1152]{1,0:T(8,128)(2,1)}), bf16[256,1152]{1,0:T(8,128)(2,1)}) %reduce-scatter.13.cloned.1.call-update) | async-done | bytes 589840 | tf_op jit(solution)/shard_map/reduce_scatter | solution.py:95
  431.9 2.6 fusion.159
  435.0 47.1 %all-gather.15.cloned.1.call-done = bf16[2048,1152]{1,0:T(8,128)(2,1)} async-done(((bf16[256,1152]{1,0:T(8,128)(2,1)}), bf16[2048,1152]{1,0:T(8,128)(2,1)}) %all-gather.15.cloned.1.call-update) | async-done | bytes 4718608 | tf_op jit(solution)/shard_map/all_gather | solution.py:91
  482.1 8.2 fusion.51
  490.2 44.6 %all-gather.17.cloned.1.call-done = bf16[2048,1152]{1,0:T(8,128)(2,1)} async-done(((bf16[256,1152]{1,0:T(8,128)(2,1)}), bf16[2048,1152]{1,0:T(8,128)(2,1)}) %all-gather.17.cloned.1.call-update) | async-done | bytes 4718608 | tf_op jit(solution)/shard_map/all_gather | solution.py:101
  534.8 9.9 fusion.178
  546.2 5.8 convolution_convert_fusion.3
  552.2 10.0 convolution_convert_fusion.4
  562.3 43.6 %reduce-scatter.17.cloned.1.call-done = bf16[256,1152]{1,0:T(8,128)(2,1)} async-done(((bf16[2048,1152]{1,0:T(8,128)(2,1)}), bf16[256,1152]{1,0:T(8,128)(2,1)}) %reduce-scatter.17.cloned.1.call-update) | async-done | bytes 589840 | tf_op jit(solution)/shard_map/reduce_scatter | solution.py:105
  605.9 2.1 fusion.74
  609.3 52.7 %reduce-scatter.15.cloned.1.call-done = bf16[256,1152]{1,0:T(8,128)(2,1)} async-done(((bf16[2048,1152]{1,0:T(8,128)(2,1)}), bf16[256,1152]{1,0:T(8,128)(2,1)}) %reduce-scatter.15.cloned.1.call-update) | async-done | bytes 589840 | tf_op jit(solution)/shard_map/reduce_scatter | solution.py:95
  662.0 2.7 fusion.164
  667.7 50.0 %all-gather.19.cloned.1.call-done = bf16[2048,1152]{1,0:T(8,128)(2,1)} async-done(((bf16[256,1152]{1,0:T(8,128)(2,1)}), bf16[2048,1152]{1,0:T(8,128)(2,1)}) %all-gather.19.cloned.1.call-update) | async-done | bytes 4718608 | tf_op jit(solution)/shard_map/all_gather | solution.py:101
  717.7 4.0 convolution_convert_fusion.17
  723.7 4.3 fusion.174
  731.7 2.3 fusion.175
  744.6 4.6 convolution_convert_fusion.1
  749.3 53.9 %reduce-scatter.19.cloned.1.call-done = bf16[256,1152]{1,0:T(8,128)(2,1)} async-done(((bf16[2048,1152]{1,0:T(8,128)(2,1)}), bf16[256,1152]{1,0:T(8,128)(2,1)}) %reduce-scatter.19.cloned.1.call-update) | async-done | bytes 589840 | tf_op jit(solution)/shard_map/reduce_scatter | solution.py:105
  805.2 2.2 fusion.75
  807.6 2.5 fusion.158
  810.4 49.9 %all-gather.21.cloned.1.call-done = bf16[2048,1152]{1,0:T(8,128)(2,1)} async-done(((bf16[256,1152]{1,0:T(8,128)(2,1)}), bf16[2048,1152]{1,0:T(8,128)(2,1)}) %all-gather.21.cloned.1.call-update) | async-done | bytes 4718608 | tf_op jit(solution)/shard_map/all_gather | solution.py:101
  860.3 9.9 fusion.179
  871.6 5.8 convolution_convert_fusion.2
  877.5 53.9 %reduce-scatter.21.cloned.1.call-done = bf16[256,1152]{1,0:T(8,128)(2,1)} async-done(((bf16[2048,1152]{1,0:T(8,128)(2,1)}), bf16[256,1152]{1,0:T(8,128)(2,1)}) %reduce-scatter.21.cloned.1.call-update) | async-done | bytes 589840 | tf_op jit(solution)/shard_map/reduce_scatter | solution.py:105
  931.4 2.4 fusion.76
  937.0 49.7 %all-gather.23.cloned.1.call-done = bf16[2048,1152]{1,0:T(8,128)(2,1)} async-done(((bf16[256,1152]{1,0:T(8,128)(2,1)}), bf16[2048,1152]{1,0:T(8,128)(2,1)}) %all-gather.23.cloned.1.call-update) | async-done | bytes 4718608 | tf_op jit(solution)/shard_map/all_gather | solution.py:101
  986.8 4.1 convolution_convert_fusion.16
  999.2 4.6 convolution_convert_fusion
  1005.0 7.3 fusion.22
  1012.4 9.2 fusion.20
  1024.0 2.6 fusion.79
  1026.6 3.5 fusion.24
  1030.2 5.9 convolution_convert_fusion.12
  1038.2 6.4 fusion.21
  1046.4 8.2 fusion.19
  1056.7 3.5 fusion.23
  1061.1 4.9 convolution_convert_fusion.13
  1074.2 26.9 %all-reduce = (bf16[2,6912]{1,0:T(2,128)(2,1)S(1)}, bf16[2,1152]{1,0:T(2,128)(2,1)S(1)}, bf16[2,1152]{1,0:T(2,128)(2,1)S(1)}) all-reduce(bf16[2,6912]{1,0:T(2,128)(2,1)S(1)} %pad_maximum_fusion.4, bf16[2,1152]{1,0:T(2,128)(2,1)S(1)} %get-tuple-element.108, ...), channel_id=1, replica_groups=mesh['dp'=4,'tensor'=8] {'tensor'}, use_global_device_ids=true, to_apply=%region_43.44 | all-reduce | flops 18432 | bytes 73728 | tf_op jit(solution)/shard_map/psum | solution.py:299
  1101.1 2.5 multiply_convert_fusion
  1104.6 3.2 fusion.128
  1108.5 18.3 %all-reduce.1 = (bf16[2,6912]{1,0:T(2,128)(2,1)S(1)}, bf16[2,2,144]{2,1,0:T(2,128)(2,1)S(1)}, bf16[2,1152]{1,0:T(2,128)(2,1)S(1)}, bf16[2,576]{1,0:T(2,128)(2,1)S(1)}, bf16[2,1152]{1,0:T(2,128)(2,1)S(1)}) all-reduce(bf16[2,6912]{1,0:T(2,128)(2,1)S(1)} %get-tuple-element.41, ...), channel_id=1, replica_groups=mesh['dp'=4,'tensor'=8] {'dp'}, use_global_device_ids=true, to_apply=%region_45.46 | all-reduce | flops 20160 | bytes 80640 | tf_op jit(solution)/shard_map/psum | solution.py:312
  1129.9 206.3 %all-reduce.5.cloned.1.call-done = (bf16[2,144,6912]{2,1,0:T(8,128)(2,1)}, bf16[2,1152,3,144]{1,3,2,0:T(8,128)(2,1)}, bf16[2,144,1152]{2,1,0:T(8,128)(2,1)}, bf1...) async-done(((bf16[2,144,6912]{2,1,0:T(8,128)(2,1)}, bf16[2,1152,3,144]{1,3,2,0:T(8,128)(2,1)}, bf16[2,144,1152]{2,1,0:T(8,128)(2,1)}, bf16[2,1152,576]{1,2,0:T(8,128)(2,1)}, ...) | async-done | bytes 11943952 | tf_op jit(solution)/shard_map/psum | solution.py:311
  1336.2 2.2 convert_element_type.435
  1338.4 6.0 convert_element_type.427
  1344.5 2.2 convert_element_type.429
  1347.5 2.7 convert_element_type.439
  1350.4 2.7 convert_element_type.443
  (423 shorter events, 100.0 us)
Async XLA Ops:
  7.2 89.7 %all-gather.9.cloned.1.call-start = ((), (), s32[]{:S(2)}) async-start(), calls=%async_computation.8 | async-start | bytes 5308416 | tf_op jit(solution)/shard_map/all_gather | solution.py:91
  7.9 6.0 copy-start.105
  9.1 36.5 %copy-start.66 = (f32[256]{0:T(256)}, f32[256]{0:T(256)S(1)}, u32[]{:S(2)}) copy-start(f32[256]{0:T(256)S(1)} %broadcast_multiply_fusion.3) | copy-start | bytes 3076
  10.5 35.1 %copy-start.78 = (f32[256]{0:T(256)}, f32[256]{0:T(256)S(1)}, u32[]{:S(2)}) copy-start(f32[256]{0:T(256)S(1)} %fusion.137) | copy-start | bytes 3076
  11.1 33.7 %copy-start.68 = (bf16[2,6912]{1,0:T(2,128)(2,1)S(1)}, bf16[2,6912]{1,0:T(2,128)(2,1)}, u32[]{:S(2)}) copy-start(bf16[2,6912]{1,0:T(2,128)(2,1)} %param.16) | copy-start | bytes 82948
  11.1 34.5 %copy-start = (bf16[1,256,1152]{2,1,0:T(8,128)(2,1)S(1)}, bf16[1,256,1152]{2,1,0:T(8,128)(2,1)}, u32[]{:S(2)}) copy-start(bf16[1,256,1152]{2,1,0:T(8,128)(2,1)} %param.13) | copy-start | bytes 1769476
  13.9 32.9 %copy-start.107 = (bf16[2,2,144]{2,1,0:T(2,128)(2,1)S(1)}, bf16[2,2,144]{2,1,0:T(2,128)(2,1)}, u32[]{:S(2)}) copy-start(bf16[2,2,144]{2,1,0:T(2,128)(2,1)} %param.18) | copy-start | bytes 3460
  13.9 32.9 %copy-start.30 = (bf16[2,1152,3,144]{1,3,2,0:T(8,128)(2,1)S(1)}, bf16[2,1152,3,144]{1,3,2,0:T(8,128)(2,1)}, u32[]{:S(2)}) copy-start(bf16[2,1152,3,144]{1,3,2,0:T(8,128)(2,1)} %param.17) | copy-start | bytes 5971972
  45.6 125.8 %copy-start.54 = (f32[1152]{0:T(1024)}, f32[1152]{0:T(1024)S(1)}, u32[]{:S(2)}) copy-start(f32[1152]{0:T(1024)S(1)} %get-tuple-element.30) | copy-start | bytes 13828
  45.6 245.9 %copy-start.59 = (f32[1152]{0:T(1024)}, f32[1152]{0:T(1024)S(1)}, u32[]{:S(2)}) copy-start(f32[1152]{0:T(1024)S(1)} %get-tuple-element.31) | copy-start | bytes 13828
  45.6 247.8 %copy-start.48 = (f32[1152]{0:T(1024)}, f32[1152]{0:T(1024)S(1)}, u32[]{:S(2)}) copy-start(f32[1152]{0:T(1024)S(1)} %get-tuple-element.27) | copy-start | bytes 13828
  46.8 121.7 %reduce-scatter.9.cloned.1.call-start = ((), (), s32[]{:S(2)}) async-start(), calls=%async_computation.9 | async-start | bytes 5308416 | tf_op jit(solution)/shard_map/reduce_scatter | solution.py:95
  114.6 108.4 %all-gather.11.cloned.1.call-start = ((), (), s32[]{:S(2)}) async-start(), calls=%async_computation.10 | async-start | bytes 5308416 | tf_op jit(solution)/shard_map/all_gather | solution.py:91
  169.9 58.7 %copy-start.69 = (f32[256]{0:T(256)}, f32[256]{0:T(256)S(1)}, u32[]{:S(2)}) copy-start(f32[256]{0:T(256)S(1)} %broadcast_multiply_fusion.2) | copy-start | bytes 3076
  171.4 57.2 %copy-start.101 = (f32[256]{0:T(256)}, f32[256]{0:T(256)S(1)}, u32[]{:S(2)}) copy-start(f32[256]{0:T(256)S(1)} %multiply_reduce_fusion.9) | copy-start | bytes 3076
  171.4 57.2 %copy-start.80 = (f32[256]{0:T(256)}, f32[256]{0:T(256)S(1)}, u32[]{:S(2)}) copy-start(f32[256]{0:T(256)S(1)} %fusion.138) | copy-start | bytes 3076
  172.7 118.8 %reduce-scatter.11.cloned.1.call-start = ((), (), s32[]{:S(2)}) async-start(), calls=%async_computation.11 | async-start | bytes 5308416 | tf_op jit(solution)/shard_map/reduce_scatter | solution.py:95
  173.6 55.0 %copy-start.109 = (f32[576]{0:T(1024)}, f32[576]{0:T(1024)S(1)}, u32[]{:S(2)}) copy-start(f32[576]{0:T(1024)S(1)} %get-tuple-element.40) | copy-start | bytes 6916
  223.0 7.9 copy-start.116
  237.6 107.1 %all-gather.13.cloned.1.call-start = ((), (), s32[]{:S(2)}) async-start(), calls=%async_computation.12 | async-start | bytes 5308416 | tf_op jit(solution)/shard_map/all_gather | solution.py:91
  238.9 55.6 %copy-start.57 = (f32[1152]{0:T(1024)}, f32[1152]{0:T(1024)S(1)}, u32[]{:S(2)}) copy-start(f32[1152]{0:T(1024)S(1)} %get-tuple-element.36) | copy-start | bytes 13828
  293.0 51.7 %copy-start.37 = (bf16[1,1152,3,144]{1,3,2,0:T(8,128)(2,1)S(1)}, bf16[1,1152,3,144]{1,3,2,0:T(8,128)(2,1)}, u32[]{:S(2)}) copy-start(bf16[1,1152,3,144]{1,3,2,0:T(8,128)(2,1)} %get-tuple-element.78) | copy-start | bytes 2985988
  293.1 56.5 %copy-start.64 = (f32[256]{0:T(256)}, f32[256]{0:T(256)S(1)}, u32[]{:S(2)}) copy-start(f32[256]{0:T(256)S(1)} %broadcast_multiply_fusion.1) | copy-start | bytes 3076
  293.3 56.2 %copy-start.103 = (f32[256]{0:T(256)}, f32[256]{0:T(256)S(1)}, u32[]{:S(2)}) copy-start(f32[256]{0:T(256)S(1)} %multiply_reduce_fusion.8) | copy-start | bytes 3076
  293.4 56.2 %copy-start.76 = (f32[256]{0:T(256)}, f32[256]{0:T(256)S(1)}, u32[]{:S(2)}) copy-start(f32[256]{0:T(256)S(1)} %fusion.139) | copy-start | bytes 3076
  294.5 132.8 %reduce-scatter.13.cloned.1.call-start = ((), (), s32[]{:S(2)}) async-start(), calls=%async_computation.13 | async-start | bytes 5308416 | tf_op jit(solution)/shard_map/reduce_scatter | solution.py:95
  373.4 108.7 %all-gather.15.cloned.1.call-start = ((), (), s32[]{:S(2)}) async-start(), calls=%async_computation.14 | async-start | bytes 5308416 | tf_op jit(solution)/shard_map/all_gather | solution.py:91
  431.9 103.0 %all-gather.17.cloned.1.call-start = ((), (), s32[]{:S(2)}) async-start(), calls=%async_computation.16 | async-start | bytes 5308416 | tf_op jit(solution)/shard_map/all_gather | solution.py:101
  434.5 171.4 %reduce-scatter.17.cloned.1.call-start = ((), (), s32[]{:S(2)}) async-start(), calls=%async_computation.17 | async-start | bytes 5308416 | tf_op jit(solution)/shard_map/reduce_scatter | solution.py:105
  534.8 11.3 copy-start.117
  552.0 110.0 %reduce-scatter.15.cloned.1.call-start = ((), (), s32[]{:S(2)}) async-start(), calls=%async_computation.15 | async-start | bytes 5308416 | tf_op jit(solution)/shard_map/reduce_scatter | solution.py:95
  562.3 155.4 %all-gather.19.cloned.1.call-start = ((), (), s32[]{:S(2)}) async-start(), calls=%async_computation.18 | async-start | bytes 5308416 | tf_op jit(solution)/shard_map/all_gather | solution.py:101
  664.7 53.0 %copy-start.41 = (bf16[2,144,1152]{2,1,0:T(8,128)(2,1)S(1)}, bf16[2,144,1152]{2,1,0:T(8,128)(2,1)}, u32[]{:S(2)}) copy-start(bf16[2,144,1152]{2,1,0:T(8,128)(2,1)} %param.19) | copy-start | bytes 1990660
  664.7 53.0 %copy-start.82 = (f32[256]{0:T(256)}, f32[256]{0:T(256)S(1)}, u32[]{:S(2)}) copy-start(f32[256]{0:T(256)S(1)} %negate_multiply_fusion.3) | copy-start | bytes 3076
  667.5 135.6 %reduce-scatter.19.cloned.1.call-start = ((), (), s32[]{:S(2)}) async-start(), calls=%async_computation.19 | async-start | bytes 5308416 | tf_op jit(solution)/shard_map/reduce_scatter | solution.py:105
  749.2 58.3 %copy-start.3 = (f32[256,1152]{1,0:T(8,128)S(1)}, f32[256,1152]{1,0:T(8,128)}, u32[]{:S(2)}) copy-start(f32[256,1152]{1,0:T(8,128)} %copy-done.2) | copy-start | bytes 3538948
  749.2 111.1 %all-gather.21.cloned.1.call-start = ((), (), s32[]{:S(2)}) async-start(), calls=%async_computation.20 | async-start | bytes 5308416 | tf_op jit(solution)/shard_map/all_gather | solution.py:101
  810.1 121.3 %reduce-scatter.21.cloned.1.call-start = ((), (), s32[]{:S(2)}) async-start(), calls=%async_computation.21 | async-start | bytes 5308416 | tf_op jit(solution)/shard_map/reduce_scatter | solution.py:105
  860.3 11.3 copy-start.118
  877.4 54.0 %copy-start.55 = (f32[1152]{0:T(1024)S(1)}, f32[1152]{0:T(1024)}, u32[]{:S(2)}) copy-start(f32[1152]{0:T(1024)} %copy-done.54) | copy-start | bytes 13828
  877.4 54.0 %copy-start.70 = (f32[256]{0:T(256)S(1)}, f32[256]{0:T(256)}, u32[]{:S(2)}) copy-start(f32[256]{0:T(256)} %copy-done.69) | copy-start | bytes 3076
  877.4 54.0 %copy-start.81 = (f32[256]{0:T(256)S(1)}, f32[256]{0:T(256)}, u32[]{:S(2)}) copy-start(f32[256]{0:T(256)} %copy-done.80) | copy-start | bytes 3076
  877.4 56.3 %copy-start.102 = (f32[256]{0:T(256)S(1)}, f32[256]{0:T(256)}, u32[]{:S(2)}) copy-start(f32[256]{0:T(256)} %copy-done.101) | copy-start | bytes 3076
  877.5 56.9 %copy-start.7 = (f32[256,1152]{1,0:T(8,128)S(1)}, f32[256,1152]{1,0:T(8,128)}, u32[]{:S(2)}) copy-start(f32[256,1152]{1,0:T(8,128)} %get-tuple-element.58) | copy-start | bytes 3538948
  877.5 109.3 %all-gather.23.cloned.1.call-start = ((), (), s32[]{:S(2)}) async-start(), calls=%async_computation.22 | async-start | bytes 5308416 | tf_op jit(solution)/shard_map/all_gather | solution.py:101
  934.4 52.4 %copy-start.42 = (bf16[2,144,1152]{2,1,0:T(8,128)(2,1)S(1)}, bf16[2,144,1152]{2,1,0:T(8,128)(2,1)}, u32[]{:S(2)}) copy-start(bf16[2,144,1152]{2,1,0:T(8,128)(2,1)} %param.19) | copy-start | bytes 1990660
  936.5 54.5 %copy-start.63 = (f32[8,2,256]{2,1,0:T(2,128)S(1)}, f32[8,2,256]{2,1,0:T(2,128)}, u32[]{:S(2)}) copy-start(f32[8,2,256]{2,1,0:T(2,128)} %copy-done.62) | copy-start | bytes 49156
  936.5 130.9 %reduce-scatter.23.cloned.1.call-start = ((), (), s32[]{:S(2)}) async-start(), calls=%async_computation.23 | async-start | bytes 5308416 | tf_op jit(solution)/shard_map/reduce_scatter | solution.py:105
  1003.8 332.4 %all-reduce.5.cloned.1.call-start = ((), (), s32[]{:S(2)}) async-start(), calls=%async_computation.24 | async-start | bytes 23887872 | tf_op jit(solution)/shard_map/psum | solution.py:311
  1005.0 7.3 copy-start.111
  1012.4 9.2 copy-start.93
  1012.4 11.6 copy-start.4
  1012.4 11.6 copy-start.56
  1030.1 6.3 copy-start.87
  1030.1 6.5 copy-start.91
  1030.1 6.8 copy-start.90
  1030.1 7.1 copy-start.85
  1030.2 7.3 copy-start.89
  1030.2 7.8 copy-start.28
  1030.2 7.8 copy-start.58
  1038.2 6.5 copy-start.33
  1046.4 8.2 copy-start.32
  1070.9 30.2 %copy-start.108 = (f32[144]{0:T(256)S(1)}, f32[144]{0:T(256)}, u32[]{:S(2)}) copy-start(f32[144]{0:T(256)} %get-tuple-element.54) | copy-start | bytes 1732
  1338.4 6.0 copy-start.31
  (77 other events, 201.4 us)
Sparse Core Ops, SparseCore 0:
  46.9 49.9 all-gather.8
  114.7 53.7 reduce-scatter.8
  172.9 50.0 all-gather.10
  237.7 53.7 reduce-scatter.10
  294.6 50.0 all-gather.12
  373.5 53.7 reduce-scatter.12
  432.0 50.0 all-gather.14
  484.3 50.5 all-gather.16
  552.1 53.7 reduce-scatter.16
  608.7 53.3 reduce-scatter.14
  667.6 50.0 all-gather.18
  749.3 53.7 reduce-scatter.18
  810.2 50.0 all-gather.20
  877.6 53.7 reduce-scatter.20
  936.6 50.0 all-gather.22
  1003.9 53.7 reduce-scatter.22
  1103.7 232.4 all-reduce.4
where the time goes:
time: 1370 us; the launch traced here: 1360 us
  waiting for transfers between devices  959 us (70%)
  matrix products  176 us (13%)
  other arithmetic  82.1 us (6%)
  blocking collectives  76 us (6%)
  local copies, waits for them, and re-layouts  48.3 us (4%)
  between operations  16 us (1%)
    reduce_scatter x4, waiting for transfers between devices, reduce_rows(): lax.psum_scatter(partial_terms.astype(jnp.bfloat16), 'tensor', scatter_di...  212 us
    psum x1, waiting for transfers between devices, per_device(): lax.psum(ada_w_grad.astype(jnp.bfloat16), 'dp').astype(jnp.float32)  206 us
    all_gather x4, waiting for transfers between devices, spread_rows(): return lax.all_gather(row_block, 'tensor', axis=0, tiled=True)  195 us
    all_gather x4, waiting for transfers between devices, spread_grads(): return lax.all_gather(row_block, 'tensor', axis=0, tiled=True)  194 us
    reduce_scatter x4, waiting for transfers between devices, reduce_grads(): lax.psum_scatter(partial_terms.astype(jnp.bfloat16), 'tensor', scatter_di...  151 us
    psum x1, blocking collectives, per_device(): modulations = lax.psum(ada_terms, 'tensor') + ada_bias.astype(jnp.float32)  30.9 us
    unnamed x278, local copies, waits for them, and re-layouts  27.9 us
  transfers between devices with their start and end apart: 17, of which 16 were waited for; matrix products, arithmetic and copies ran while one was open for 7% of the time, Pallas kernels for 0%

commit v1 on v0

--- a/solution.py
+++ b/solution.py
@@ -3,7 +3,7 @@
 import jax
 import jax.numpy as jnp
 from jax import lax
-from jax.sharding import PartitionSpec as P
+from jax.sharding import Mesh, PartitionSpec as P
 
 HEAD_DIM = 72
 PATCHES = 256
@@ -336,37 +336,427 @@
     )
 
 
+LINE = ("z", "c")
+PLANE = ("y", "x")
+
+
+def swap(value, axis):
+    return lax.ppermute(value, axis, [(0, 1), (1, 0)])
+
+
+def pick(value, index, axis=0):
+    return lax.dynamic_index_in_dim(value, index, axis, keepdims=False)
+
+
+def gather_attention(qkv_w, out_w):
+    me_c = lax.axis_index("c")
+    me = 2 * lax.axis_index("y") + lax.axis_index("x")
+    mine = pick(jnp.concatenate([jnp.transpose(qkv_w, (1, 2, 0)), out_w[None]]), me)
+    whole = lax.all_gather(mine, LINE, axis=0).reshape((4, 2) + mine.shape)
+    half = pick(whole, me_c, 1)
+    from_x = swap(half, "x")
+    from_y = swap(half, "y")
+    from_xy = swap(from_x, "y")
+    result = jnp.zeros((4,) + whole.shape, whole.dtype)
+    result = lax.dynamic_update_slice(result, whole[None], (me, 0, 0, 0, 0))
+    for flip, part in ((1, from_x), (2, from_y), (3, from_xy)):
+        other = swap(part, "c")
+        result = lax.dynamic_update_slice(
+            result, part[None, :, None], (me ^ flip, 0, me_c, 0, 0)
+        )
+        result = lax.dynamic_update_slice(
+            result, other[None, :, None], (me ^ flip, 0, 1 - me_c, 0, 0)
+        )
+    return result
+
+
+def gather_hidden(piece):
+    me_c = lax.axis_index("c")
+    whole = lax.all_gather(piece, LINE, axis=0).reshape((4, 2) + piece.shape)
+    part = swap(pick(whole, me_c, 1), "y")
+    other = swap(part, "c")
+    width = piece.shape[-1]
+    return jnp.concatenate(
+        [whole.reshape(-1, width), part.reshape(-1, width), other.reshape(-1, width)]
+    )
+
+
+def hidden_order(quarters):
+    me_c = lax.axis_index("c")
+    me = 2 * lax.axis_index("y") + lax.axis_index("x")
+    near = pick(quarters, me ^ 2, 2)
+    return jnp.concatenate(
+        [
+            pick(quarters, me, 2).reshape(-1),
+            pick(near, me_c, 1).reshape(-1),
+            pick(near, 1 - me_c, 1).reshape(-1),
+        ]
+    )
+
+
+def hidden_place(values):
+    me_c = lax.axis_index("c")
+    me = 2 * lax.axis_index("y") + lax.axis_index("x")
+    count = values.shape[0] // 16
+    own = values[: 8 * count].reshape(4, 2, 1, count)
+    part = values[8 * count : 12 * count].reshape(4, 1, 1, count)
+    other = values[12 * count :].reshape(4, 1, 1, count)
+    result = jnp.zeros((4, 2, 4, count), values.dtype)
+    result = lax.dynamic_update_slice(result, own, (0, 0, me, 0))
+    result = lax.dynamic_update_slice(result, part, (0, me_c, me ^ 2, 0))
+    return lax.dynamic_update_slice(result, other, (0, 1 - me_c, me ^ 2, 0))
+
+
+def reduce_line(blocks):
+    mine = lax.psum_scatter(blocks, "z", scatter_dimension=0, tiled=False)
+    return lax.all_gather(mine, PLANE, axis=0)
+
+
+def reduce_attention(grads):
+    me_c, me_x, me_y = lax.axis_index("c"), lax.axis_index("x"), lax.axis_index("y")
+    low = jnp.bfloat16
+    kept = pick(grads, me_c, 2) + swap(pick(grads, 1 - me_c, 2), "c")
+    kept = kept.reshape((2, 2) + kept.shape[1:])
+    kept = pick(kept, me_y) + swap(pick(kept, 1 - me_y), "y")
+    kept = pick(kept, me_x) + swap(pick(kept, 1 - me_x), "x")
+    return reduce_line(kept.astype(low))
+
+
+def reduce_hidden(grads):
+    me_c = lax.axis_index("c")
+    rows, width = grads.shape[0] // 16, grads.shape[1]
+    own = grads[: 8 * rows].reshape(4, 2, rows, width)
+    part = grads[8 * rows : 12 * rows].reshape(4, rows, width)
+    other = grads[12 * rows :].reshape(4, rows, width)
+    part = part + swap(other, "c")
+    own = pick(own, me_c, 1) + swap(pick(own, 1 - me_c, 1), "c")
+    return reduce_line(own + swap(part, "y")).reshape(4 * rows, width)
+
+
+def to_heads(rows):
+    return rows.reshape(rows.shape[0], -1, HEAD_DIM)
+
+
+def local_probs(query, key, mask):
+    scores = jnp.einsum(
+        "qhd,khd->hqk", to_heads(query), to_heads(key), preferred_element_type=jnp.float32
+    ) * HEAD_DIM ** (-0.5)
+    if mask is not None:
+        scores = jnp.where(mask, scores, -jnp.inf)
+    return jax.nn.softmax(scores, axis=-1)
+
+
+def local_attend(query, key, value, mask):
+    probs = local_probs(query, key, mask).astype(jnp.bfloat16)
+    mixed = jnp.einsum("hqk,khd->qhd", probs, to_heads(value), preferred_element_type=jnp.float32)
+    return mixed.reshape(query.shape).astype(jnp.bfloat16)
+
+
+def local_attend_back(query, key, value, grad, mask):
+    probs = local_probs(query, key, mask)
+    value_grad = jnp.einsum(
+        "hqk,qhd->khd",
+        probs.astype(jnp.bfloat16),
+        to_heads(grad),
+        preferred_element_type=jnp.float32,
+    )
+    probs_grad = jnp.einsum(
+        "qhd,khd->hqk", to_heads(grad), to_heads(value), preferred_element_type=jnp.float32
+    )
+    score_grad = probs * (probs_grad - jnp.sum(probs_grad * probs, axis=-1, keepdims=True))
+    score_low = score_grad.astype(jnp.bfloat16)
+    factor = HEAD_DIM ** (-0.5)
+    query_grad = (
+        jnp.einsum("hqk,khd->qhd", score_low, to_heads(key), preferred_element_type=jnp.float32)
+        * factor
+    )
+    key_grad = (
+        jnp.einsum("hqk,qhd->khd", score_low, to_heads(query), preferred_element_type=jnp.float32)
+        * factor
+    )
+    return tuple(
+        part.reshape(query.shape).astype(jnp.bfloat16)
+        for part in (query_grad, key_grad, value_grad)
+    )
+
+
+def rows_dot(left, right):
+    return jnp.einsum("tk,rk->tr", left, right, preferred_element_type=jnp.float32)
+
+
+def weight_grad(left, right):
+    return jnp.einsum("tr,td->rd", left, right, preferred_element_type=jnp.float32).astype(
+        jnp.bfloat16
+    )
+
+
+def block_forward(stream, modulation, weights, biases, mask):
+    qkvo, fc1, fc2 = weights
+    query_b, value_b, out_b, fc1_b, fc2_b = biases
+    shift_att, scale_att, gate_att, shift_mlp, scale_mlp, gate_mlp = jnp.split(modulation, 6)
+    width = stream.shape[1]
+    matrices = qkvo.reshape(4 * width, width)
+    normed = modulate(stream, shift_att, scale_att).astype(jnp.bfloat16)
+    projected = rows_dot(normed, matrices[: 3 * width])
+    query = (projected[:, :width] + query_b).astype(jnp.bfloat16)
+    key = projected[:, width : 2 * width].astype(jnp.bfloat16)
+    value = (projected[:, 2 * width :] + value_b).astype(jnp.bfloat16)
+    heads_out = local_attend(query, key, value, mask)
+    attn_branch = (
+        jnp.dot(heads_out, matrices[3 * width :], preferred_element_type=jnp.float32) + out_b
+    )
+    middle = stream + gate_att * attn_branch
+    normed_mlp = modulate(middle, shift_mlp, scale_mlp).astype(jnp.bfloat16)
+    both = (normed_mlp, swap(normed_mlp, "x"))
+    hidden = [rows_dot(part, fc1) + fc1_b for part in both]
+    activated = [jax.nn.gelu(part, approximate=True).astype(jnp.bfloat16) for part in hidden]
+    terms = [jnp.dot(part, fc2, preferred_element_type=jnp.float32) for part in activated]
+    mlp_branch = terms[0] + swap(terms[1].astype(jnp.bfloat16), "x").astype(jnp.float32) + fc2_b
+    result = middle + gate_mlp * mlp_branch
+    saved = (
+        normed,
+        query,
+        key,
+        value,
+        heads_out,
+        attn_branch,
+        middle,
+        both,
+        hidden,
+        activated,
+        mlp_branch,
+    )
+    return result, saved
+
+
+def block_backward(stream, modulation, weights, saved, stream_grad, mask):
+    qkvo, fc1, fc2 = weights
+    (
+        normed,
+        query,
+        key,
+        value,
+        heads_out,
+        attn_branch,
+        middle,
+        both,
+        hidden,
+        activated,
+        mlp_branch,
+    ) = saved
+    shift_att, scale_att, gate_att, shift_mlp, scale_mlp, gate_mlp = jnp.split(modulation, 6)
+    width = stream.shape[1]
+    matrices = qkvo.reshape(4 * width, width)
+    mlp_grad = (gate_mlp * stream_grad).astype(jnp.bfloat16)
+    gate_mlp_grad = jnp.sum(stream_grad * mlp_branch, axis=0)
+    fc2_b_grad = jnp.sum(mlp_grad, axis=0, dtype=jnp.float32)
+    mlp_grads = (mlp_grad, swap(mlp_grad, "x"))
+    hidden_grads = []
+    for part, grad in zip(hidden, mlp_grads):
+        _, gelu_back = jax.vjp(partial(jax.nn.gelu, approximate=True), part)
+        hidden_grads.append(gelu_back(rows_dot(grad, fc2))[0].astype(jnp.bfloat16))
+    terms = [jnp.dot(part, fc1, preferred_element_type=jnp.float32) for part in hidden_grads]
+    mlp_in_grad = terms[0] + swap(terms[1].astype(jnp.bfloat16), "x").astype(jnp.float32)
+    hidden_grad = jnp.concatenate(hidden_grads)
+    fc1_b_grad = jnp.sum(hidden_grad, axis=0, dtype=jnp.float32)
+    fc2_grad = weight_grad(jnp.concatenate(activated), jnp.concatenate(mlp_grads))
+    fc1_grad = weight_grad(hidden_grad, jnp.concatenate(both))
+    _, mlp_norm_back = jax.vjp(modulate, middle, shift_mlp, scale_mlp)
+    middle_part, shift_mlp_grad, scale_mlp_grad = mlp_norm_back(mlp_in_grad)
+    middle_grad = stream_grad + middle_part
+    attn_grad = (gate_att * middle_grad).astype(jnp.bfloat16)
+    gate_att_grad = jnp.sum(middle_grad * attn_branch, axis=0)
+    out_b_grad = jnp.sum(attn_grad, axis=0, dtype=jnp.float32)
+    out_grad = weight_grad(heads_out, attn_grad)
+    heads_grad = rows_dot(attn_grad, matrices[3 * width :]).astype(jnp.bfloat16)
+    qkv_grads = local_attend_back(query, key, value, heads_grad, mask)
+    qkv_grad = jnp.concatenate(qkv_grads, axis=1)
+    qkv_w_grad = weight_grad(qkv_grad, normed)
+    qkvo_grad = jnp.concatenate([qkv_w_grad, out_grad]).reshape(qkvo.shape)
+    attn_in_grad = jnp.dot(qkv_grad, matrices[: 3 * width], preferred_element_type=jnp.float32)
+    _, att_norm_back = jax.vjp(modulate, stream, shift_att, scale_att)
+    stream_part, shift_att_grad, scale_att_grad = att_norm_back(attn_in_grad)
+    input_grad = middle_grad + stream_part
+    small = jnp.concatenate(
+        [
+            shift_att_grad,
+            scale_att_grad,
+            gate_att_grad,
+            shift_mlp_grad,
+            scale_mlp_grad,
+            gate_mlp_grad,
+            jnp.sum(qkv_grads[0], axis=0, dtype=jnp.float32),
+            jnp.sum(qkv_grads[2], axis=0, dtype=jnp.float32),
+            out_b_grad,
+            fc2_b_grad,
+            hidden_place(fc1_b_grad).reshape(-1),
+        ]
+    )
+    small = lax.all_gather(lax.psum(small, LINE), PLANE, axis=0)
+    return (
+        input_grad,
+        small,
+        reduce_attention(qkvo_grad),
+        reduce_hidden(fc1_grad),
+        reduce_hidden(fc2_grad),
+    )
+
+
+def frame_parallel(
+    latents,
+    conditioning,
+    ada_weight,
+    ada_bias,
+    qkv_weight,
+    qkv_bias,
+    out_weight,
+    out_bias,
+    fc1_weight,
+    fc1_bias,
+    fc2_weight,
+    fc2_bias,
+    out_grad,
+):
+    me = 2 * lax.axis_index("y") + lax.axis_index("x")
+    block = 2 * lax.axis_index("z") + lax.axis_index("c")
+    width = latents.shape[2]
+    tokens = latents.shape[1]
+
+    def reshard(value):
+        return lax.all_to_all(value, LINE, 0, 0, tiled=True)
+
+    silu_out, silu_back = jax.vjp(jax.nn.silu, conditioning[0].astype(jnp.float32))
+    silu_cond = silu_out.astype(jnp.bfloat16)
+    ada_terms = jnp.einsum("d,ldm->lm", silu_cond, ada_weight, preferred_element_type=jnp.float32)
+    modulations = lax.psum(ada_terms, LINE) + ada_bias.astype(jnp.float32)
+
+    quarter = fc1_bias.shape[1] // 4
+    weights = []
+    for layer in range(LAYERS):
+        fc1_rows = jnp.transpose(
+            lax.dynamic_slice_in_dim(fc1_weight[layer], me * quarter, quarter, 1)
+        )
+        fc2_rows = lax.dynamic_slice_in_dim(fc2_weight[layer], me * quarter, quarter, 0)
+        weights.append(
+            (
+                gather_attention(qkv_weight[layer], out_weight[layer]),
+                gather_hidden(fc1_rows),
+                gather_hidden(fc2_rows),
+            )
+        )
+    head_width = qkv_bias.shape[2]
+    small = jnp.concatenate([qkv_bias.reshape(LAYERS, -1), fc1_bias], axis=1)
+    small = lax.all_gather(small, LINE, axis=0).astype(jnp.float32)
+    biases = []
+    for layer in range(LAYERS):
+        part = small[:, layer]
+        biases.append(
+            (
+                part[:, :head_width].reshape(-1),
+                part[:, head_width : 2 * head_width].reshape(-1),
+                out_bias[layer].astype(jnp.float32),
+                hidden_order(part[:, 2 * head_width :].reshape(4, 2, 4, quarter)),
+                fc2_bias[layer].astype(jnp.float32),
+            )
+        )
+
+    patch = jnp.arange(tokens) % (PATCHES // 8)
+    masks = [None, patch[:, None] == patch[None, :]]
+    stream = latents[0].astype(jnp.float32)
+    inputs_kept, saved_all = [], []
+    for layer in range(LAYERS):
+        if layer:
+            stream = reshard(stream.astype(jnp.bfloat16)).astype(jnp.float32)
+        inputs_kept.append(stream)
+        stream, saved = block_forward(
+            stream, modulations[layer], weights[layer], biases[layer], masks[layer]
+        )
+        saved_all.append(saved)
+    layer_output = reshard(stream.astype(jnp.bfloat16))[None]
+
+    stream_grad = reshard(out_grad[0]).astype(jnp.float32)
+    results = [None] * LAYERS
+    for layer in reversed(range(LAYERS)):
+        stream_grad, *results[layer] = block_backward(
+            inputs_kept[layer],
+            modulations[layer],
+            weights[layer],
+            saved_all[layer],
+            stream_grad,
+            masks[layer],
+        )
+        if layer:
+            stream_grad = reshard(stream_grad.astype(jnp.bfloat16)).astype(jnp.float32)
+
+    smalls = jnp.stack([member[0] for member in results])
+    mod_all = smalls[:, :, : 6 * width].astype(jnp.bfloat16)
+    sums = jnp.sum(smalls[:, :, 6 * width :], axis=1)
+    silu_all = lax.all_gather(silu_cond, PLANE, axis=0)
+    ada_w_grad = jnp.einsum("bk,lbm->lkm", silu_all, mod_all, preferred_element_type=jnp.float32)
+    ada_b_grad = jnp.sum(mod_all.astype(jnp.float32), axis=1)
+    silu_grad = jnp.einsum(
+        "lm,ldm->d", pick(mod_all, me, 1), ada_weight, preferred_element_type=jnp.float32
+    )
+    cond_grad = silu_back(silu_grad)[0]
+    qkv_b_grad = pick(sums[:, : 2 * width].reshape(LAYERS, 2, 8, head_width), block, 2)
+    fc1_b_grad = pick(sums[:, 4 * width :].reshape(LAYERS, 8, 4 * quarter), block, 1)
+    attention = jnp.stack([member[1] for member in results]).astype(jnp.float32)
+    return (
+        layer_output,
+        stream_grad.astype(jnp.bfloat16)[None],
+        cond_grad.astype(jnp.bfloat16)[None],
+        ada_w_grad,
+        ada_b_grad,
+        jnp.transpose(attention[:, :3], (0, 3, 1, 2)),
+        qkv_b_grad,
+        attention[:, 3],
+        sums[:, 2 * width : 3 * width],
+        jnp.transpose(
+            jnp.stack([member[2] for member in results]).astype(jnp.float32), (0, 2, 1)
+        ),
+        fc1_b_grad,
+        jnp.stack([member[3] for member in results]).astype(jnp.float32),
+        sums[:, 3 * width : 4 * width],
+    )
+
+
 def solution(mesh):
+    dp, tensor = mesh.shape["dp"], mesh.shape["tensor"]
+    if dp == 4 and tensor == 8:
+        split = Mesh(mesh.devices.reshape(2, 2, 4, 2), ("y", "x", "z", "c"))
+        return sharded(split, frame_parallel, ("y", "x"), ("z", "c"))
+    return sharded(mesh, per_device, "dp", "tensor")
+
+
+def sharded(mesh, body, dp, tensor):
     in_specs = (
-        P("dp", "tensor", None),
-        P("dp", "tensor"),
-        P(None, "tensor", None),
+        P(dp, tensor, None),
+        P(dp, tensor),
+        P(None, tensor, None),
         P(),
-        P(None, None, None, "tensor"),
-        P(None, None, "tensor"),
-        P(None, "tensor", None),
+        P(None, None, None, tensor),
+        P(None, None, tensor),
+        P(None, tensor, None),
         P(),
-        P(None, None, "tensor"),
-        P(None, "tensor"),
-        P(None, "tensor", None),
+        P(None, None, tensor),
+        P(None, tensor),
+        P(None, tensor, None),
         P(),
-        P("dp", "tensor", None),
+        P(dp, tensor, None),
     )
     out_specs = (
-        P("dp", "tensor", None),
-        P("dp", "tensor", None),
-        P("dp", "tensor"),
-        P(None, "tensor", None),
+        P(dp, tensor, None),
+        P(dp, tensor, None),
+        P(dp, tensor),
+        P(None, tensor, None),
         P(),
-        P(None, None, None, "tensor"),
-        P(None, None, "tensor"),
-        P(None, "tensor", None),
+        P(None, None, None, tensor),
+        P(None, None, tensor),
+        P(None, tensor, None),
         P(),
-        P(None, None, "tensor"),
-        P(None, "tensor"),
-        P(None, "tensor", None),
+        P(None, None, tensor),
+        P(None, tensor),
+        P(None, tensor, None),
         P(),
     )
-    return jax.shard_map(
-        per_device, mesh=mesh, in_specs=in_specs, out_specs=out_specs, check_vma=False
-    )
+    return jax.shard_map(body, mesh=mesh, in_specs=in_specs, out_specs=out_specs, check_vma=False)

time: 1370 us -> 1210 us (0.88)
  waiting for transfers between devices: 959 us -> 596 us
  local copies, waits for them, and re-layouts: 48.3 us -> 172 us
  starting transfers between devices: 2.6 us -> 53.2 us
  other arithmetic: 82.1 us -> 103 us
    reduce_scatter x8 -> x6, waiting for transfers between devices: 363 us -> 9.48 us  [reduce_line(): mine = lax.psum_scatter(blocks, 'z', scatter_dimension=0, tiled=False)]
    ppermute x0 -> x46, waiting for transfers between devices: none -> 286 us  [swap(): return lax.ppermute(value, axis, [(0, 1), (1, 0)])]
    psum x1, waiting for transfers between devices: 206 us -> 5.74 us  [block_backward(): small = lax.all_gather(lax.psum(small, LINE), PLANE, axis=0)]
    all_gather x8 -> x12, waiting for transfers between devices: 389 us -> 279 us  [the longest x6 169 us: reduce_line(): return lax.all_gather(mine, PLANE, axis=0)]
    all_gather x0 -> x4, blocking collectives: none -> 40 us  [the longest x2 17.6 us: block_backward(): small = lax.all_gather(lax.psum(small, LINE), PLANE, axis=0)]
    add x4 -> x18, other arithmetic: 1.87 us -> 41.2 us  [the longest x4 11.3 us: reduce_hidden(): return reduce_line(own + swap(part, 'y')).reshape(4 * rows, width)]
    slice x3 -> x31, local copies, waits for them, and re-layouts: 1.57 us -> 39.6 us  [the longest x2 14.2 us: block_forward(): projected = rows_dot(normed, matrices[:3 * width])]
    psum x3 -> x1, blocking collectives: 76 us -> 41.5 us  [frame_parallel(): modulations = lax.psum(ada_terms, LINE) + ada_bias.astype(jnp.float32)]
  transfers between devices with their start and end apart: 17 -> 69, of which waited for: 16 -> 29; matrix products, arithmetic and copies ran while one was open for 7% -> 33% of each run, Pallas kernels for 0% -> 0%
where the time goes in v1:
time: 1210 us; the launch traced here: 1200 us
  waiting for transfers between devices  596 us (49%)
  matrix products  183 us (15%)
  local copies, waits for them, and re-layouts  172 us (14%)
  other arithmetic  103 us (9%)
  blocking collectives  81.6 us (7%)
  starting transfers between devices  53.2 us (4%)
  between operations  16.7 us (1%)
    ppermute x46, waiting for transfers between devices, swap(): return lax.ppermute(value, axis, [(0, 1), (1, 0)])  286 us
    all_gather x6, waiting for transfers between devices, reduce_line(): return lax.all_gather(mine, PLANE, axis=0)  169 us
    all_gather x4, waiting for transfers between devices, gather_hidden(): whole = lax.all_gather(piece, LINE, axis=0).reshape((4, 2) + piece.shape)  109 us
    dot_general x12, matrix products, rows_dot(): jnp.einsum('tk,rk->tr', left, right, preferred_element_type=jnp.float32)  69.9 us
    psum x1, blocking collectives, frame_parallel(): modulations = lax.psum(ada_terms, LINE) + ada_bias.astype(jnp.float32)  41.5 us
    squeeze x16, local copies, waits for them, and re-layouts, pick(): return lax.dynamic_index_in_dim(value, index, axis, keepdims=False)  34.1 us
    ppermute x46, starting transfers between devices, swap(): return lax.ppermute(value, axis, [(0, 1), (1, 0)])  32.7 us
    concatenate x2, other arithmetic, block_backward(): qkvo_grad = jnp.concatenate([qkv_w_grad, out_grad]).reshape(qkvo.shape)  29.5 us
  transfers between devices with their start and end apart: 69, of which 29 were waited for; matrix products, arithmetic and copies ran while one was open for 33% of the time, Pallas kernels for 0%

profile of v1, /device:TPU:0, one launch (start us, length us, event | category | flops | bytes accessed | tf_op | source)
XLA Modules:
  0.0 1204.8 jit_solution(6591806201061324214)
XLA Ops:
  18.8 6.3 all-to-all-start.2
  30.5 41.5 %psum.21 = f32[2,6912]{1,0:T(2,128)S(1)} all-reduce(f32[2,6912]{1,0:T(2,128)S(1)} %bitcast.500), channel_id=1, replica_groups=mesh['y'=2,'x'=2,'z'=4,'c'=2] {'z','c'}, use_global_device_ids=true, to_apply=%region_0.1 | all-reduce | flops 13824 | bytes 110592 | tf_op jit(solution)/shard_map/psum | solution.py:631
  72.2 14.5 %all-gather.3 = bf16[8,2,864]{2,1,0:T(2,128)(2,1)S(1)} all-gather(bf16[1,2,864]{2,1,0:T(2,128)(2,1)S(1)} %maximum_bitcast_fusion), channel_id=2, replica_groups=mesh['y'=2,'x'=2,'z'=4,'c'=2] {'z','c'}, dimensions={0}, use_global_device_ids=true | all-gather | bytes 31104 | tf_op jit(solution)/shard_map/all_gather | solution.py:649
  104.2 26.9 %all-gather.40.cloned.1.call-done = bf16[1152,1152]{1,0:T(8,128)(2,1)} async-done(((bf16[144,1152]{1,0:T(8,128)(2,1)}), bf16[1152,1152]{1,0:T(8,128)(2,1)}) %all-gather.40.cloned.1.call-update) | async-done | bytes 2654224 | tf_op jit(solution)/shard_map/all_gather | solution.py:375
  135.0 31.3 %all-gather.22.cloned.1.call-done = bf16[8,144,1152]{2,1,0:T(8,128)(2,1)} async-done(((bf16[1,144,1152]{2,1,0:T(8,128)(2,1)}), bf16[8,144,1152]{2,1,0:T(8,128)(2,1)}) %all-gather.22.cloned.1.call-update) | async-done | bytes 2654224 | tf_op jit(solution)/shard_map/all_gather | solution.py:375
  168.8 4.8 broadcast.284.clone
  175.3 25.7 %all-gather.42.cloned.1.call-done = bf16[1152,1152]{1,0:T(8,128)(2,1)} async-done(((bf16[144,1152]{1,0:T(8,128)(2,1)}), bf16[1152,1152]{1,0:T(8,128)(2,1)}) %all-gather.42.cloned.1.call-update) | async-done | bytes 2654224 | tf_op jit(solution)/shard_map/all_gather | solution.py:375
  203.5 4.8 broadcast.284.clone.1
  210.2 25.4 %all-gather.26.cloned.1.call-done = bf16[8,144,1152]{2,1,0:T(8,128)(2,1)} async-done(((bf16[1,144,1152]{2,1,0:T(8,128)(2,1)}), bf16[8,144,1152]{2,1,0:T(8,128)(2,1)}) %all-gather.26.cloned.1.call-update) | async-done | bytes 2654224 | tf_op jit(solution)/shard_map/all_gather | solution.py:375
  249.4 23.4 %collective-permute-done.4 = bf16[4,144,1152]{2,1,0:T(8,128)(2,1)S(1)} collective-permute-done((bf16[4,144,1152]{2,1,0:T(8,128)(2,1)}, bf16[4,144,1152]{2,1,0:T(8,128)(2,1)S(1)}, u32[]{:S(2)}, u32[]{:S(2)}) %collective-permute-start.4) | collective-permute-done | bytes 1327136 | tf_op jit(solution)/shard_map/ppermute | solution.py:344
  279.6 7.1 slice.323
  288.7 6.8 fusion.116
  304.0 5.0 fusion.195
  316.5 13.3 %collective-permute-done.18 = bf16[4,144,1152]{2,1,0:T(8,128)(2,1)} collective-permute-done((bf16[4,144,1152]{2,1,0:T(8,128)(2,1)}, bf16[4,144,1152]{2,1,0:T(8,128)(2,1)}, u32[]{:S(2)}, u32[]{:S(2)}) %collective-permute-start.18) | collective-permute-done | bytes 1327136 | tf_op jit(solution)/shard_map/ppermute | solution.py:344
  336.3 21.9 %collective-permute-done.20 = bf16[4,144,1152]{2,1,0:T(8,128)(2,1)} collective-permute-done((bf16[4,144,1152]{2,1,0:T(8,128)(2,1)}, bf16[4,144,1152]{2,1,0:T(8,128)(2,1)}, u32[]{:S(2)}, u32[]{:S(2)}) %collective-permute-start.20) | collective-permute-done | bytes 1327136 | tf_op jit(solution)/shard_map/ppermute | solution.py:344
  359.8 26.1 %collective-permute-done.16 = bf16[4,144,1152]{2,1,0:T(8,128)(2,1)S(1)} collective-permute-done((bf16[4,144,1152]{2,1,0:T(8,128)(2,1)S(1)}, bf16[4,144,1152]{2,1,0:T(8,128)(2,1)S(1)}, u32[]{:S(2)}, u32[]{:S(2)}) %collective-permute-start.16) | collective-permute-done | bytes 1327136 | tf_op jit(solution)/shard_map/ppermute | solution.py:344
  386.4 6.2 multiply_convert_fusion.4
  398.1 6.2 multiply_convert_fusion.5
  404.4 7.6 collective-permute-done.11
  422.6 7.1 slice.332
  438.3 5.9 fusion.198
  462.7 6.7 multiply_convert_fusion.3
  469.5 7.3 fusion.28
  476.8 6.2 multiply_convert_fusion.2
  487.3 4.8 convolution_convert_fusion.2
  494.0 7.0 fusion.35
  501.0 5.2 convolution_convert_fusion.4
  534.1 5.2 multiply_reduce_fusion.3
  558.1 6.0 fusion.92
  571.9 13.9 %pad_maximum_fusion.1 = bf16[4608,1152]{1,0:T(8,128)(2,1)S(1)} fusion(bf16[1152,1152]{1,0:T(8,128)(2,1)S(1)} %convolution_convert_fusion.6, bf16[3456,1152]{1,0:T(8,128)(2,1)S(1)} %convolution_convert_fusion), kind=kLoop, calls=%fused_computation.9 | loop fusion | flops 21233664 | bytes 21233664 | tf_op jit(solution)/shard_map/concatenate | solution.py:575
  598.1 8.4 fusion.14
  606.5 6.4 collective-permute-done.26
  621.0 6.3 fusion.21
  634.9 8.4 collective-permute-done.45
  646.6 10.3 collective-permute-done.27
  656.9 5.8 multiply_reduce_fusion.5
  683.3 15.5 %pad_maximum_fusion = bf16[4608,1152]{1,0:T(8,128)(2,1)} fusion(bf16[1152,1152]{1,0:T(8,128)(2,1)S(1)} %convolution_convert_fusion.7, bf16[3456,1152]{1,0:T(8,128)(2,1)S(1)} %convolution_convert_fusion.1), kind=kLoop, calls=%fused_computation.8 | loop fusion | flops 21233664 | bytes 21233664 | tf_op jit(solution)/shard_map/concatenate | solution.py:575
  698.9 14.4 %collective-permute-done.42 = bf16[4,144,1152]{2,1,0:T(8,128)(2,1)S(1)} collective-permute-done((bf16[4,144,1152]{2,1,0:T(8,128)(2,1)S(1)}, bf16[4,144,1152]{2,1,0:T(8,128)(2,1)S(1)}, u32[]{:S(2)}, u32[]{:S(2)}) %collective-permute-start.42) | collective-permute-done | bytes 1327136 | tf_op jit(solution)/shard_map/ppermute | solution.py:344
  716.1 5.4 dynamic-slice_bitcast_fusion.1
  733.7 21.4 %collective-permute-done.39 = bf16[4,144,1152]{2,1,0:T(8,128)(2,1)S(1)} collective-permute-done((bf16[4,144,1152]{2,1,0:T(8,128)(2,1)S(1)}, bf16[4,144,1152]{2,1,0:T(8,128)(2,1)S(1)}, u32[]{:S(2)}, u32[]{:S(2)}) %collective-permute-start.39) | collective-permute-done | bytes 1327136 | tf_op jit(solution)/shard_map/ppermute | solution.py:344
  762.3 4.9 bitcast_add_fusion
  773.4 19.9 %collective-permute-done.36 = bf16[4,144,1152]{2,1,0:T(8,128)(2,1)} collective-permute-done((bf16[4,144,1152]{2,1,0:T(8,128)(2,1)}, bf16[4,144,1152]{2,1,0:T(8,128)(2,1)}, u32[]{:S(2)}, u32[]{:S(2)}) %collective-permute-start.36) | collective-permute-done | bytes 1327136 | tf_op jit(solution)/shard_map/ppermute | solution.py:344
  797.0 4.7 bitcast_add_fusion.1
  806.3 43.9 %collective-permute-done.32 = bf16[2,4,144,1152]{3,2,1,0:T(8,128)(2,1)} collective-permute-done((bf16[2,4,144,1152]{3,2,1,0:T(8,128)(2,1)}, bf16[2,4,144,1152]{3,2,1,0:T(8,128)(2,1)}, u32[]{:S(2)}, u32[]{:S(2)}) %collective-permute-start.32) | collective-permute-done | bytes 2654240 | tf_op jit(solution)/shard_map/ppermute | solution.py:344
  854.5 5.9 fusion.66
  862.0 20.0 %collective-permute-done.33 = bf16[4,144,1152]{2,1,0:T(8,128)(2,1)S(1)} collective-permute-done((bf16[4,144,1152]{2,1,0:T(8,128)(2,1)S(1)}, bf16[4,144,1152]{2,1,0:T(8,128)(2,1)S(1)}, u32[]{:S(2)}, u32[]{:S(2)}) %collective-permute-start.33) | collective-permute-done | bytes 1327136 | tf_op jit(solution)/shard_map/ppermute | solution.py:344
  883.4 22.4 %collective-permute-done.29 = bf16[2,4,144,1152]{3,2,1,0:T(8,128)(2,1)} collective-permute-done((bf16[2,4,144,1152]{3,2,1,0:T(8,128)(2,1)}, bf16[2,4,144,1152]{3,2,1,0:T(8,128)(2,1)}, u32[]{:S(2)}, u32[]{:S(2)}) %collective-permute-start.29) | collective-permute-done | bytes 2654240 | tf_op jit(solution)/shard_map/ppermute | solution.py:344
  914.5 25.8 %collective-permute-done.30 = bf16[4,144,1152]{2,1,0:T(8,128)(2,1)} collective-permute-done((bf16[4,144,1152]{2,1,0:T(8,128)(2,1)}, bf16[4,144,1152]{2,1,0:T(8,128)(2,1)}, u32[]{:S(2)}, u32[]{:S(2)}) %collective-permute-start.30) | collective-permute-done | bytes 1327136 | tf_op jit(solution)/shard_map/ppermute | solution.py:344
  946.2 5.7 all-to-all-start.1
  952.0 8.0 all-gather.6
  960.0 9.8 all-to-all-done.1
  969.8 5.7 all-reduce.3.cloned.1.call-done
  975.5 9.3 all-gather.5
  984.9 8.3 all-gather.4
  999.0 9.4 reduce-scatter.7.cloned.1.call-done
  1009.0 4.5 convolution_bitcast_fusion
  1014.1 23.9 %all-gather.38.cloned.1.call-done = bf16[4,144,1152]{2,1,0:T(8,128)(2,1)} async-done(((bf16[1,144,1152]{2,1,0:T(8,128)(2,1)}), bf16[4,144,1152]{2,1,0:T(8,128)(2,1)}) %all-gather.38.cloned.1.call-update) | async-done | bytes 1327120 | tf_op jit(solution)/shard_map/all_gather | solution.py:412
  1038.0 30.8 %all-gather.36.cloned.1.call-done = bf16[4,144,1152]{2,1,0:T(8,128)(2,1)} async-done(((bf16[1,144,1152]{2,1,0:T(8,128)(2,1)}), bf16[4,144,1152]{2,1,0:T(8,128)(2,1)}) %all-gather.36.cloned.1.call-update) | async-done | bytes 1327120 | tf_op jit(solution)/shard_map/all_gather | solution.py:412
  1068.9 4.4 maximum_convert_fusion.1
  1073.3 26.4 %all-gather.34.cloned.1.call-done = bf16[4,144,1152]{2,1,0:T(8,128)(2,1)} async-done(((bf16[1,144,1152]{2,1,0:T(8,128)(2,1)}), bf16[4,144,1152]{2,1,0:T(8,128)(2,1)}) %all-gather.34.cloned.1.call-update) | async-done | bytes 1327120 | tf_op jit(solution)/shard_map/all_gather | solution.py:412
  1099.7 30.8 %all-gather.32.cloned.1.call-done = bf16[4,144,1152]{2,1,0:T(8,128)(2,1)} async-done(((bf16[1,144,1152]{2,1,0:T(8,128)(2,1)}), bf16[4,144,1152]{2,1,0:T(8,128)(2,1)}) %all-gather.32.cloned.1.call-update) | async-done | bytes 1327120 | tf_op jit(solution)/shard_map/all_gather | solution.py:412
  1130.5 4.4 convert_bitcast_fusion
  1135.0 26.4 %all-gather.30.cloned.1.call-done = bf16[4,144,1152]{2,1,0:T(8,128)(2,1)} async-done(((bf16[1,144,1152]{2,1,0:T(8,128)(2,1)}), bf16[4,144,1152]{2,1,0:T(8,128)(2,1)}) %all-gather.30.cloned.1.call-update) | async-done | bytes 1327120 | tf_op jit(solution)/shard_map/all_gather | solution.py:412
  1161.3 31.0 %all-gather.28.cloned.1.call-done = bf16[4,144,1152]{2,1,0:T(8,128)(2,1)} async-done(((bf16[1,144,1152]{2,1,0:T(8,128)(2,1)}), bf16[4,144,1152]{2,1,0:T(8,128)(2,1)}) %all-gather.28.cloned.1.call-update) | async-done | bytes 1327120 | tf_op jit(solution)/shard_map/all_gather | solution.py:412
  (717 shorter events, 318.8 us)
Async XLA Ops:
  7.2 88.0 %all-gather.20.cloned.1.call-start = ((), (), s32[]{:S(2)}) async-start(), calls=%async_computation.10 | async-start | bytes 2985984 | tf_op jit(solution)/shard_map/all_gather | solution.py:355
  9.9 90.7 %all-gather.24.cloned.1.call-start = ((), (), s32[]{:S(2)}) async-start(), calls=%async_computation.12 | async-start | bytes 2985984 | tf_op jit(solution)/shard_map/all_gather | solution.py:355
  10.9 120.2 %all-gather.40.cloned.1.call-start = ((), (), s32[]{:S(2)}) async-start(), calls=%async_computation.26 | async-start | bytes 2985984 | tf_op jit(solution)/shard_map/all_gather | solution.py:375
  14.9 151.5 %all-gather.22.cloned.1.call-start = ((), (), s32[]{:S(2)}) async-start(), calls=%async_computation.11 | async-start | bytes 2985984 | tf_op jit(solution)/shard_map/all_gather | solution.py:375
  17.0 184.0 %all-gather.42.cloned.1.call-start = ((), (), s32[]{:S(2)}) async-start(), calls=%async_computation.27 | async-start | bytes 2985984 | tf_op jit(solution)/shard_map/all_gather | solution.py:375
  18.8 74.6 %all-to-all-start.2 = ((bf16[8,32,1152]{2,1,0:T(8,128)(2,1)}), bf16[8,32,1152]{2,1,0:T(8,128)(2,1)S(1)}, u32[]{:S(2)}, u32[]{:S(2)}) async-start(bf16[8,32,1152]{2,1,0:T(8,128)(2,1)} %bitcast.80), calls=%async_computation.2 | async-start | bytes 1179648 | tf_op jit(solution)/shard_map/all_to_all | solution.py:626
  25.1 210.5 %all-gather.26.cloned.1.call-start = ((), (), s32[]{:S(2)}) async-start(), calls=%async_computation.13 | async-start | bytes 2985984 | tf_op jit(solution)/shard_map/all_gather | solution.py:375
  97.6 112.4 %collective-permute-start = (bf16[4,144,1152]{2,1,0:T(8,128)(2,1)}, bf16[4,144,1152]{2,1,0:T(8,128)(2,1)}, u32[]{:S(2)}, u32[]{:S(2)}) collective-permute-start(bf16[4,144,1152]{2,1,0:T(8,128)(2,1)} %dynamic-slice_bitcast_fusion.15), channel_id=1, source_target_pairs={{0,8},{8,0},{1,9},{9,1},{2,10},{10,2},{3,11},{11,3},{4,12},{12,4},... | collective-permute-start | bytes 3981320 | tf_op jit(solution)/shard_map/ppermute | solution.py:344
  99.1 141.5 %collective-permute-start.2 = (bf16[4,144,1152]{2,1,0:T(8,128)(2,1)}, bf16[4,144,1152]{2,1,0:T(8,128)(2,1)}, u32[]{:S(2)}, u32[]{:S(2)}) collective-permute-start(bf16[4,144,1152]{2,1,0:T(8,128)(2,1)} %dynamic-slice_bitcast_fusion.15), channel_id=1, source_target_pairs={{0,16},{16,0},{1,17},{17,1},{2,18},{18,2},{3,19},{19,3},{4,20},{20... | collective-permute-start | bytes 3981320 | tf_op jit(solution)/shard_map/ppermute | solution.py:344
  103.1 139.1 %collective-permute-start.12 = (bf16[4,144,1152]{2,1,0:T(8,128)(2,1)}, bf16[4,144,1152]{2,1,0:T(8,128)(2,1)S(1)}, u32[]{:S(2)}, u32[]{:S(2)}) collective-permute-start(bf16[4,144,1152]{2,1,0:T(8,128)(2,1)} %dynamic-slice_bitcast_fusion.12), channel_id=1, source_target_pairs={{0,8},{8,0},{1,9},{9,1},{2,10},{10,2},{3,11},{11,3},{4,12},{12,4},... | collective-permute-start | bytes 3981320 | tf_op jit(solution)/shard_map/ppermute | solution.py:344
  103.6 174.2 %collective-permute-start.14 = (bf16[4,144,1152]{2,1,0:T(8,128)(2,1)}, bf16[4,144,1152]{2,1,0:T(8,128)(2,1)}, u32[]{:S(2)}, u32[]{:S(2)}) collective-permute-start(bf16[4,144,1152]{2,1,0:T(8,128)(2,1)} %dynamic-slice_bitcast_fusion.12), channel_id=1, source_target_pairs={{0,16},{16,0},{1,17},{17,1},{2,18},{18,2},{3,19},{19,3},{4,20},{20... | collective-permute-start | bytes 3981320 | tf_op jit(solution)/shard_map/ppermute | solution.py:344
  133.6 180.9 %collective-permute-start.6 = (bf16[4,144,1152]{2,1,0:T(8,128)(2,1)}, bf16[4,144,1152]{2,1,0:T(8,128)(2,1)}, u32[]{:S(2)}, u32[]{:S(2)}) collective-permute-start(bf16[4,144,1152]{2,1,0:T(8,128)(2,1)} %dynamic-slice_bitcast_fusion.14), channel_id=1, source_target_pairs={{0,16},{16,0},{1,17},{17,1},{2,18},{18,2},{3,19},{19,3},{4,20},{20... | collective-permute-start | bytes 3981320 | tf_op jit(solution)/shard_map/ppermute | solution.py:344
  210.0 33.5 %collective-permute-start.1 = (bf16[4,144,1152]{2,1,0:T(8,128)(2,1)}, bf16[4,144,1152]{2,1,0:T(8,128)(2,1)}, u32[]{:S(2)}, u32[]{:S(2)}) collective-permute-start(bf16[4,144,1152]{2,1,0:T(8,128)(2,1)} %collective-permute-done), channel_id=1, source_target_pairs={{0,1},{1,0},{2,3},{3,2},{4,5},{5,4},{6,7},{7,6},{8,9},{9,8},{10,11... | collective-permute-start | bytes 3981320 | tf_op jit(solution)/shard_map/ppermute | solution.py:344
  240.6 32.2 %collective-permute-start.4 = (bf16[4,144,1152]{2,1,0:T(8,128)(2,1)}, bf16[4,144,1152]{2,1,0:T(8,128)(2,1)S(1)}, u32[]{:S(2)}, u32[]{:S(2)}) collective-permute-start(bf16[4,144,1152]{2,1,0:T(8,128)(2,1)} %collective-permute-done), channel_id=1, source_target_pairs={{0,16},{16,0},{1,17},{17,1},{2,18},{18,2},{3,19},{19,3},{4,20},{20... | collective-permute-start | bytes 3981320 | tf_op jit(solution)/shard_map/ppermute | solution.py:344
  243.5 31.7 %collective-permute-start.13 = (bf16[4,144,1152]{2,1,0:T(8,128)(2,1)S(1)}, bf16[4,144,1152]{2,1,0:T(8,128)(2,1)S(1)}, u32[]{:S(2)}, u32[]{:S(2)}) collective-permute-start(bf16[4,144,1152]{2,1,0:T(8,128)(2,1)S(1)} %collective-permute-done.12), channel_id=1, source_target_pairs={{0,1},{1,0},{2,3},{3,2},{4,5},{5,4},{6,7},{7,6},{8,9},{9,8},{10,11... | collective-permute-start | bytes 3981320 | tf_op jit(solution)/shard_map/ppermute | solution.py:344
  248.9 67.1 %collective-permute-start.8 = (bf16[4,144,1152]{2,1,0:T(8,128)(2,1)}, bf16[4,144,1152]{2,1,0:T(8,128)(2,1)}, u32[]{:S(2)}, u32[]{:S(2)}) collective-permute-start(bf16[4,144,1152]{2,1,0:T(8,128)(2,1)} %dynamic-slice_bitcast_fusion.13), channel_id=1, source_target_pairs={{0,16},{16,0},{1,17},{17,1},{2,18},{18,2},{3,19},{19,3},{4,20},{20... | collective-permute-start | bytes 3981320 | tf_op jit(solution)/shard_map/ppermute | solution.py:344
  275.2 54.6 %collective-permute-start.18 = (bf16[4,144,1152]{2,1,0:T(8,128)(2,1)}, bf16[4,144,1152]{2,1,0:T(8,128)(2,1)}, u32[]{:S(2)}, u32[]{:S(2)}) collective-permute-start(bf16[4,144,1152]{2,1,0:T(8,128)(2,1)} %dynamic-slice_bitcast_fusion.11), channel_id=1, source_target_pairs={{0,16},{16,0},{1,17},{17,1},{2,18},{18,2},{3,19},{19,3},{4,20},{20... | collective-permute-start | bytes 3981320 | tf_op jit(solution)/shard_map/ppermute | solution.py:344
  277.8 80.4 %collective-permute-start.20 = (bf16[4,144,1152]{2,1,0:T(8,128)(2,1)}, bf16[4,144,1152]{2,1,0:T(8,128)(2,1)}, u32[]{:S(2)}, u32[]{:S(2)}) collective-permute-start(bf16[4,144,1152]{2,1,0:T(8,128)(2,1)} %dynamic-slice_bitcast_fusion.10), channel_id=1, source_target_pairs={{0,16},{16,0},{1,17},{17,1},{2,18},{18,2},{3,19},{19,3},{4,20},{20... | collective-permute-start | bytes 3981320 | tf_op jit(solution)/shard_map/ppermute | solution.py:344
  278.4 51.4 %collective-permute-start.15 = (bf16[4,144,1152]{2,1,0:T(8,128)(2,1)}, bf16[4,144,1152]{2,1,0:T(8,128)(2,1)}, u32[]{:S(2)}, u32[]{:S(2)}) collective-permute-start(bf16[4,144,1152]{2,1,0:T(8,128)(2,1)} %collective-permute-done.14), channel_id=1, source_target_pairs={{0,1},{1,0},{2,3},{3,2},{4,5},{5,4},{6,7},{7,6},{8,9},{9,8},{10,11... | collective-permute-start | bytes 3981320 | tf_op jit(solution)/shard_map/ppermute | solution.py:344
  314.4 71.5 %collective-permute-start.16 = (bf16[4,144,1152]{2,1,0:T(8,128)(2,1)S(1)}, bf16[4,144,1152]{2,1,0:T(8,128)(2,1)S(1)}, u32[]{:S(2)}, u32[]{:S(2)}) collective-permute-start(bf16[4,144,1152]{2,1,0:T(8,128)(2,1)S(1)} %copy-done.49), channel_id=1, source_target_pairs={{0,16},{16,0},{1,17},{17,1},{2,18},{18,2},{3,19},{19,3},{4,20},{20... | collective-permute-start | bytes 3981320 | tf_op jit(solution)/shard_map/ppermute | solution.py:344
  316.0 43.8 %collective-permute-start.7 = (bf16[4,144,1152]{2,1,0:T(8,128)(2,1)}, bf16[4,144,1152]{2,1,0:T(8,128)(2,1)S(1)}, u32[]{:S(2)}, u32[]{:S(2)}) collective-permute-start(bf16[4,144,1152]{2,1,0:T(8,128)(2,1)} %collective-permute-done.6), channel_id=1, source_target_pairs={{0,1},{1,0},{2,3},{3,2},{4,5},{5,4},{6,7},{7,6},{8,9},{9,8},{10,11... | collective-permute-start | bytes 3981320 | tf_op jit(solution)/shard_map/ppermute | solution.py:344
  329.8 62.8 %collective-permute-start.9 = (bf16[4,144,1152]{2,1,0:T(8,128)(2,1)}, bf16[4,144,1152]{2,1,0:T(8,128)(2,1)S(1)}, u32[]{:S(2)}, u32[]{:S(2)}) collective-permute-start(bf16[4,144,1152]{2,1,0:T(8,128)(2,1)} %collective-permute-done.8), channel_id=1, source_target_pairs={{0,1},{1,0},{2,3},{3,2},{4,5},{5,4},{6,7},{7,6},{8,9},{9,8},{10,11... | collective-permute-start | bytes 3981320 | tf_op jit(solution)/shard_map/ppermute | solution.py:344
  329.8 56.1 %collective-permute-start.10 = (bf16[256,1152]{1,0:T(8,128)(2,1)S(1)}, bf16[256,1152]{1,0:T(8,128)(2,1)S(1)}, u32[]{:S(2)}, u32[]{:S(2)}) collective-permute-start(bf16[256,1152]{1,0:T(8,128)(2,1)S(1)} %add_convert_fusion.5), channel_id=1, source_target_pairs={{0,8},{8,0},{1,9},{9,1},{2,10},{10,2},{3,11},{11,3},{4,12},{12,4},... | collective-permute-start | bytes 1769480 | tf_op jit(solution)/shard_map/ppermute | solution.py:344
  358.2 129.1 %collective-permute-start.24 = (bf16[256,1152]{1,0:T(8,128)(2,1)}, bf16[256,1152]{1,0:T(8,128)(2,1)}, u32[]{:S(2)}, u32[]{:S(2)}) collective-permute-start(bf16[256,1152]{1,0:T(8,128)(2,1)} %fusion.91), channel_id=1, source_target_pairs={{0,8},{8,0},{1,9},{9,1},{2,10},{10,2},{3,11},{11,3},{4,12},{12,4},... | collective-permute-start | bytes 1769480 | tf_op jit(solution)/shard_map/ppermute | solution.py:344
  359.8 103.0 %collective-permute-start.19 = (bf16[4,144,1152]{2,1,0:T(8,128)(2,1)}, bf16[4,144,1152]{2,1,0:T(8,128)(2,1)}, u32[]{:S(2)}, u32[]{:S(2)}) collective-permute-start(bf16[4,144,1152]{2,1,0:T(8,128)(2,1)} %collective-permute-done.18), channel_id=1, source_target_pairs={{0,1},{1,0},{2,3},{3,2},{4,5},{5,4},{6,7},{7,6},{8,9},{9,8},{10,11... | collective-permute-start | bytes 3981320 | tf_op jit(solution)/shard_map/ppermute | solution.py:344
  385.9 83.5 %collective-permute-start.21 = (bf16[4,144,1152]{2,1,0:T(8,128)(2,1)}, bf16[4,144,1152]{2,1,0:T(8,128)(2,1)}, u32[]{:S(2)}, u32[]{:S(2)}) collective-permute-start(bf16[4,144,1152]{2,1,0:T(8,128)(2,1)} %collective-permute-done.20), channel_id=1, source_target_pairs={{0,1},{1,0},{2,3},{3,2},{4,5},{5,4},{6,7},{7,6},{8,9},{9,8},{10,11... | collective-permute-start | bytes 3981320 | tf_op jit(solution)/shard_map/ppermute | solution.py:344
  385.9 35.5 %collective-permute-start.17 = (bf16[4,144,1152]{2,1,0:T(8,128)(2,1)S(1)}, bf16[4,144,1152]{2,1,0:T(8,128)(2,1)S(1)}, u32[]{:S(2)}, u32[]{:S(2)}) collective-permute-start(bf16[4,144,1152]{2,1,0:T(8,128)(2,1)S(1)} %collective-permute-done.16), channel_id=1, source_target_pairs={{0,1},{1,0},{2,3},{3,2},{4,5},{5,4},{6,7},{7,6},{8,9},{9,8},{10,11... | collective-permute-start | bytes 3981320 | tf_op jit(solution)/shard_map/ppermute | solution.py:344
  416.3 20.6 %all-to-all-start = ((bf16[8,32,1152]{2,1,0:T(8,128)(2,1)}), bf16[8,32,1152]{2,1,0:T(8,128)(2,1)S(1)}, u32[]{:S(2)}, u32[]{:S(2)}) async-start(bf16[8,32,1152]{2,1,0:T(8,128)(2,1)} %bitcast.494), calls=%async_computation | async-start | bytes 1179648 | tf_op jit(solution)/shard_map/all_to_all | solution.py:626
  459.9 16.9 %collective-permute-start.22 = (bf16[256,1152]{1,0:T(8,128)(2,1)}, bf16[256,1152]{1,0:T(8,128)(2,1)}, u32[]{:S(2)}, u32[]{:S(2)}) collective-permute-start(bf16[256,1152]{1,0:T(8,128)(2,1)} %add_convert_fusion.3), channel_id=1, source_target_pairs={{0,8},{8,0},{1,9},{9,1},{2,10},{10,2},{3,11},{11,3},{4,12},{12,4},... | collective-permute-start | bytes 1769480 | tf_op jit(solution)/shard_map/ppermute | solution.py:344
  513.9 19.7 %collective-permute-start.25 = (bf16[256,1152]{1,0:T(8,128)(2,1)}, bf16[256,1152]{1,0:T(8,128)(2,1)}, u32[]{:S(2)}, u32[]{:S(2)}) collective-permute-start(bf16[256,1152]{1,0:T(8,128)(2,1)} %convolution_convert_fusion.11), channel_id=1, source_target_pairs={{0,8},{8,0},{1,9},{9,1},{2,10},{10,2},{3,11},{11,3},{4,12},{12,4},... | collective-permute-start | bytes 1769480 | tf_op jit(solution)/shard_map/ppermute | solution.py:344
  514.5 42.3 %collective-permute-start.23 = (bf16[256,1152]{1,0:T(8,128)(2,1)}, bf16[256,1152]{1,0:T(8,128)(2,1)}, u32[]{:S(2)}, u32[]{:S(2)}) collective-permute-start(bf16[256,1152]{1,0:T(8,128)(2,1)} %convolution_convert_fusion.12), channel_id=1, source_target_pairs={{0,8},{8,0},{1,9},{9,1},{2,10},{10,2},{3,11},{11,3},{4,12},{12,4},... | collective-permute-start | bytes 1769480 | tf_op jit(solution)/shard_map/ppermute | solution.py:344
  516.0 79.7 %collective-permute-start.44 = (bf16[4,144,1152]{2,1,0:T(8,128)(2,1)}, bf16[4,144,1152]{2,1,0:T(8,128)(2,1)}, u32[]{:S(2)}, u32[]{:S(2)}) collective-permute-start(bf16[4,144,1152]{2,1,0:T(8,128)(2,1)} %bitcast.150), channel_id=1, source_target_pairs={{0,1},{1,0},{2,3},{3,2},{4,5},{5,4},{6,7},{7,6},{8,9},{9,8},{10,11... | collective-permute-start | bytes 3981320 | tf_op jit(solution)/shard_map/ppermute | solution.py:344
  517.1 117.6 %collective-permute-start.43 = (bf16[4,144,1152]{2,1,0:T(8,128)(2,1)}, bf16[4,144,1152]{2,1,0:T(8,128)(2,1)}, u32[]{:S(2)}, u32[]{:S(2)}) collective-permute-start(bf16[4,144,1152]{2,1,0:T(8,128)(2,1)} %dynamic-slice_bitcast_fusion.4), channel_id=1, source_target_pairs={{0,1},{1,0},{2,3},{3,2},{4,5},{5,4},{6,7},{7,6},{8,9},{9,8},{10,11... | collective-permute-start | bytes 3981320 | tf_op jit(solution)/shard_map/ppermute | solution.py:344
  517.7 204.0 %collective-permute-start.38 = (bf16[4,144,1152]{2,1,0:T(8,128)(2,1)}, bf16[4,144,1152]{2,1,0:T(8,128)(2,1)}, u32[]{:S(2)}, u32[]{:S(2)}) collective-permute-start(bf16[4,144,1152]{2,1,0:T(8,128)(2,1)} %bitcast.137), channel_id=1, source_target_pairs={{0,1},{1,0},{2,3},{3,2},{4,5},{5,4},{6,7},{7,6},{8,9},{9,8},{10,11... | collective-permute-start | bytes 3981320 | tf_op jit(solution)/shard_map/ppermute | solution.py:344
  533.6 199.8 %collective-permute-start.37 = (bf16[4,144,1152]{2,1,0:T(8,128)(2,1)}, bf16[4,144,1152]{2,1,0:T(8,128)(2,1)}, u32[]{:S(2)}, u32[]{:S(2)}) collective-permute-start(bf16[4,144,1152]{2,1,0:T(8,128)(2,1)} %dynamic-slice_bitcast_fusion.6), channel_id=1, source_target_pairs={{0,1},{1,0},{2,3},{3,2},{4,5},{5,4},{6,7},{7,6},{8,9},{9,8},{10,11... | collective-permute-start | bytes 3981320 | tf_op jit(solution)/shard_map/ppermute | solution.py:344
  564.2 33.2 %all-to-all-start.3 = ((bf16[8,32,1152]{2,1,0:T(8,128)(2,1)}), bf16[8,32,1152]{2,1,0:T(8,128)(2,1)S(1)}, u32[]{:S(2)}, u32[]{:S(2)}) async-start(bf16[8,32,1152]{2,1,0:T(8,128)(2,1)} %bitcast.493), calls=%async_computation.3 | async-start | bytes 1179648 | tf_op jit(solution)/shard_map/all_to_all | solution.py:626
  567.7 375.6 %reduce-scatter.17.cloned.1.call-start = ((), (), s32[]{:S(2)}) async-start(), calls=%async_computation.24 | async-start | bytes 1658880 | tf_op jit(solution)/shard_map/reduce_scatter | solution.py:411
  591.4 170.9 %collective-permute-start.31 = (bf16[4,4,144,1152]{3,2,1,0:T(8,128)(2,1)}, bf16[4,4,144,1152]{3,2,1,0:T(8,128)(2,1)}, u32[]{:S(2)}, u32[]{:S(2)}) collective-permute-start(bf16[4,4,144,1152]{3,2,1,0:T(8,128)(2,1)} %dynamic-slice_bitcast_fusion), channel_id=1, source_target_pairs={{0,1},{1,0},{2,3},{3,2},{4,5},{5,4},{6,7},{7,6},{8,9},{9,8},{10,11... | collective-permute-start | bytes 15925256 | tf_op jit(solution)/shard_map/ppermute | solution.py:344
  612.9 30.3 %collective-permute-start.45 = (bf16[4,144,1152]{2,1,0:T(8,128)(2,1)S(1)}, bf16[4,144,1152]{2,1,0:T(8,128)(2,1)S(1)}, u32[]{:S(2)}, u32[]{:S(2)}) collective-permute-start(bf16[4,144,1152]{2,1,0:T(8,128)(2,1)S(1)} %add.663), channel_id=1, source_target_pairs={{0,16},{16,0},{1,17},{17,1},{2,18},{18,2},{3,19},{19,3},{4,20},{20... | collective-permute-start | bytes 3981320 | tf_op jit(solution)/shard_map/ppermute | solution.py:344
  634.8 44.9 %collective-permute-start.41 = (bf16[4,144,1152]{2,1,0:T(8,128)(2,1)}, bf16[4,144,1152]{2,1,0:T(8,128)(2,1)}, u32[]{:S(2)}, u32[]{:S(2)}) collective-permute-start(bf16[4,144,1152]{2,1,0:T(8,128)(2,1)} %bitcast.144), channel_id=1, source_target_pairs={{0,1},{1,0},{2,3},{3,2},{4,5},{5,4},{6,7},{7,6},{8,9},{9,8},{10,11... | collective-permute-start | bytes 3981320 | tf_op jit(solution)/shard_map/ppermute | solution.py:344
  646.5 297.4 %reduce-scatter.15.cloned.1.call-start = ((), (), s32[]{:S(2)}) async-start(), calls=%async_computation.22 | async-start | bytes 1658880 | tf_op jit(solution)/shard_map/reduce_scatter | solution.py:411
  656.9 42.0 %collective-permute-start.40 = (bf16[4,144,1152]{2,1,0:T(8,128)(2,1)}, bf16[4,144,1152]{2,1,0:T(8,128)(2,1)}, u32[]{:S(2)}, u32[]{:S(2)}) collective-permute-start(bf16[4,144,1152]{2,1,0:T(8,128)(2,1)} %dynamic-slice_bitcast_fusion.5), channel_id=1, source_target_pairs={{0,1},{1,0},{2,3},{3,2},{4,5},{5,4},{6,7},{7,6},{8,9},{9,8},{10,11... | collective-permute-start | bytes 3981320 | tf_op jit(solution)/shard_map/ppermute | solution.py:344
  681.8 31.5 %collective-permute-start.42 = (bf16[4,144,1152]{2,1,0:T(8,128)(2,1)S(1)}, bf16[4,144,1152]{2,1,0:T(8,128)(2,1)S(1)}, u32[]{:S(2)}, u32[]{:S(2)}) collective-permute-start(bf16[4,144,1152]{2,1,0:T(8,128)(2,1)S(1)} %add.660), channel_id=1, source_target_pairs={{0,16},{16,0},{1,17},{17,1},{2,18},{18,2},{3,19},{19,3},{4,20},{20... | collective-permute-start | bytes 3981320 | tf_op jit(solution)/shard_map/ppermute | solution.py:344
  716.0 228.5 %reduce-scatter.13.cloned.1.call-start = ((), (), s32[]{:S(2)}) async-start(), calls=%async_computation.20 | async-start | bytes 1658880 | tf_op jit(solution)/shard_map/reduce_scatter | solution.py:411
  721.5 75.6 %collective-permute-start.28 = (bf16[4,4,144,1152]{3,2,1,0:T(8,128)(2,1)}, bf16[4,4,144,1152]{3,2,1,0:T(8,128)(2,1)}, u32[]{:S(2)}, u32[]{:S(2)}) collective-permute-start(bf16[4,4,144,1152]{3,2,1,0:T(8,128)(2,1)} %dynamic-slice_bitcast_fusion.1), channel_id=1, source_target_pairs={{0,1},{1,0},{2,3},{3,2},{4,5},{5,4},{6,7},{7,6},{8,9},{9,8},{10,11... | collective-permute-start | bytes 15925256 | tf_op jit(solution)/shard_map/ppermute | solution.py:344
  723.5 31.6 %collective-permute-start.39 = (bf16[4,144,1152]{2,1,0:T(8,128)(2,1)S(1)}, bf16[4,144,1152]{2,1,0:T(8,128)(2,1)S(1)}, u32[]{:S(2)}, u32[]{:S(2)}) collective-permute-start(bf16[4,144,1152]{2,1,0:T(8,128)(2,1)S(1)} %add.657), channel_id=1, source_target_pairs={{0,16},{16,0},{1,17},{17,1},{2,18},{18,2},{3,19},{19,3},{4,20},{20... | collective-permute-start | bytes 3981320 | tf_op jit(solution)/shard_map/ppermute | solution.py:344
  730.3 27.6 %collective-permute-start.35 = (bf16[4,144,1152]{2,1,0:T(8,128)(2,1)}, bf16[4,144,1152]{2,1,0:T(8,128)(2,1)}, u32[]{:S(2)}, u32[]{:S(2)}) collective-permute-start(bf16[4,144,1152]{2,1,0:T(8,128)(2,1)} %bitcast.131), channel_id=1, source_target_pairs={{0,1},{1,0},{2,3},{3,2},{4,5},{5,4},{6,7},{7,6},{8,9},{9,8},{10,11... | collective-permute-start | bytes 3981320 | tf_op jit(solution)/shard_map/ppermute | solution.py:344
  733.4 40.0 %collective-permute-start.34 = (bf16[4,144,1152]{2,1,0:T(8,128)(2,1)}, bf16[4,144,1152]{2,1,0:T(8,128)(2,1)}, u32[]{:S(2)}, u32[]{:S(2)}) collective-permute-start(bf16[4,144,1152]{2,1,0:T(8,128)(2,1)} %dynamic-slice_bitcast_fusion.7), channel_id=1, source_target_pairs={{0,1},{1,0},{2,3},{3,2},{4,5},{5,4},{6,7},{7,6},{8,9},{9,8},{10,11... | collective-permute-start | bytes 3981320 | tf_op jit(solution)/shard_map/ppermute | solution.py:344
  757.8 187.3 %reduce-scatter.11.cloned.1.call-start = ((), (), s32[]{:S(2)}) async-start(), calls=%async_computation.18 | async-start | bytes 1658880 | tf_op jit(solution)/shard_map/reduce_scatter | solution.py:411
  761.0 32.3 %collective-permute-start.36 = (bf16[4,144,1152]{2,1,0:T(8,128)(2,1)}, bf16[4,144,1152]{2,1,0:T(8,128)(2,1)}, u32[]{:S(2)}, u32[]{:S(2)}) collective-permute-start(bf16[4,144,1152]{2,1,0:T(8,128)(2,1)} %add.654), channel_id=1, source_target_pairs={{0,16},{16,0},{1,17},{17,1},{2,18},{18,2},{3,19},{19,3},{4,20},{20... | collective-permute-start | bytes 3981320 | tf_op jit(solution)/shard_map/ppermute | solution.py:344
  770.8 79.4 %collective-permute-start.32 = (bf16[2,4,144,1152]{3,2,1,0:T(8,128)(2,1)}, bf16[2,4,144,1152]{3,2,1,0:T(8,128)(2,1)}, u32[]{:S(2)}, u32[]{:S(2)}) collective-permute-start(bf16[2,4,144,1152]{3,2,1,0:T(8,128)(2,1)} %dynamic-slice_bitcast_fusion.2), channel_id=1, source_target_pairs={{0,16},{16,0},{1,17},{17,1},{2,18},{18,2},{3,19},{19,3},{4,20},{20... | collective-permute-start | bytes 7962632 | tf_op jit(solution)/shard_map/ppermute | solution.py:344
  796.8 148.9 %reduce-scatter.9.cloned.1.call-start = ((), (), s32[]{:S(2)}) async-start(), calls=%async_computation.16 | async-start | bytes 1658880 | tf_op jit(solution)/shard_map/reduce_scatter | solution.py:411
  804.9 100.9 %collective-permute-start.29 = (bf16[2,4,144,1152]{3,2,1,0:T(8,128)(2,1)}, bf16[2,4,144,1152]{3,2,1,0:T(8,128)(2,1)}, u32[]{:S(2)}, u32[]{:S(2)}) collective-permute-start(bf16[2,4,144,1152]{3,2,1,0:T(8,128)(2,1)} %dynamic-slice_bitcast_fusion.3), channel_id=1, source_target_pairs={{0,16},{16,0},{1,17},{17,1},{2,18},{18,2},{3,19},{19,3},{4,20},{20... | collective-permute-start | bytes 7962632 | tf_op jit(solution)/shard_map/ppermute | solution.py:344
  853.2 28.8 %collective-permute-start.33 = (bf16[4,144,1152]{2,1,0:T(8,128)(2,1)S(1)}, bf16[4,144,1152]{2,1,0:T(8,128)(2,1)S(1)}, u32[]{:S(2)}, u32[]{:S(2)}) collective-permute-start(bf16[4,144,1152]{2,1,0:T(8,128)(2,1)S(1)} %dynamic-slice_bitcast_fusion.8), channel_id=1, source_target_pairs={{0,8},{8,0},{1,9},{9,1},{2,10},{10,2},{3,11},{11,3},{4,12},{12,4},... | collective-permute-start | bytes 3981320 | tf_op jit(solution)/shard_map/ppermute | solution.py:344
  883.3 92.2 %all-reduce.3.cloned.1.call-start = ((), (), s32[]{:S(2)}) async-start(), calls=%async_computation.28 | async-start | bytes 258048 | tf_op jit(solution)/shard_map/psum | solution.py:595
  910.1 30.2 %collective-permute-start.30 = (bf16[4,144,1152]{2,1,0:T(8,128)(2,1)}, bf16[4,144,1152]{2,1,0:T(8,128)(2,1)}, u32[]{:S(2)}, u32[]{:S(2)}) collective-permute-start(bf16[4,144,1152]{2,1,0:T(8,128)(2,1)} %dynamic-slice_bitcast_fusion.9), channel_id=1, source_target_pairs={{0,8},{8,0},{1,9},{9,1},{2,10},{10,2},{3,11},{11,3},{4,12},{12,4},... | collective-permute-start | bytes 3981320 | tf_op jit(solution)/shard_map/ppermute | solution.py:344
  914.4 93.9 %reduce-scatter.7.cloned.1.call-start = ((), (), s32[]{:S(2)}) async-start(), calls=%async_computation.14 | async-start | bytes 1658880 | tf_op jit(solution)/shard_map/reduce_scatter | solution.py:411
  943.3 94.8 %all-gather.38.cloned.1.call-start = ((), (), s32[]{:S(2)}) async-start(), calls=%async_computation.25 | async-start | bytes 1658880 | tf_op jit(solution)/shard_map/all_gather | solution.py:412
  943.9 125.0 %all-gather.36.cloned.1.call-start = ((), (), s32[]{:S(2)}) async-start(), calls=%async_computation.23 | async-start | bytes 1658880 | tf_op jit(solution)/shard_map/all_gather | solution.py:412
  944.4 155.2 %all-gather.34.cloned.1.call-start = ((), (), s32[]{:S(2)}) async-start(), calls=%async_computation.21 | async-start | bytes 1658880 | tf_op jit(solution)/shard_map/all_gather | solution.py:412
  945.0 185.5 %all-gather.32.cloned.1.call-start = ((), (), s32[]{:S(2)}) async-start(), calls=%async_computation.19 | async-start | bytes 1658880 | tf_op jit(solution)/shard_map/all_gather | solution.py:412
  945.6 215.7 %all-gather.30.cloned.1.call-start = ((), (), s32[]{:S(2)}) async-start(), calls=%async_computation.17 | async-start | bytes 1658880 | tf_op jit(solution)/shard_map/all_gather | solution.py:412
  946.2 23.6 %all-to-all-start.1 = ((bf16[8,32,1152]{2,1,0:T(8,128)(2,1)}), bf16[8,32,1152]{2,1,0:T(8,128)(2,1)S(1)}, u32[]{:S(2)}, u32[]{:S(2)}) async-start(bf16[8,32,1152]{2,1,0:T(8,128)(2,1)} %bitcast.78), calls=%async_computation.1 | async-start | bytes 1179648 | tf_op jit(solution)/shard_map/all_to_all | solution.py:626
  951.9 240.4 %all-gather.28.cloned.1.call-start = ((), (), s32[]{:S(2)}) async-start(), calls=%async_computation.15 | async-start | bytes 1658880 | tf_op jit(solution)/shard_map/all_gather | solution.py:412
  (175 other events, 3588.5 us)
Sparse Core Ops, SparseCore 0:
  10.2 49.9 all-gather.19
  62.5 33.1 all-gather.23
  97.9 33.1 all-gather.39
  133.2 33.1 all-gather.21
  167.8 33.1 all-gather.41
  202.5 33.1 all-gather.25
  646.7 33.1 reduce-scatter.16
  716.1 32.5 reduce-scatter.14
  757.9 32.6 reduce-scatter.12
  796.9 32.6 reduce-scatter.10
  883.5 32.7 reduce-scatter.8
  919.1 56.4 all-reduce.2
  978.5 29.8 reduce-scatter.6
  1010.2 27.7 all-gather.37
  1039.9 28.9 all-gather.35
  1070.7 28.9 all-gather.33
  1101.5 28.9 all-gather.31
  1132.4 28.9 all-gather.29
  1163.3 28.9 all-gather.27
